TPU v7x, 256 devices: a whole 4x4x8 slice. The times are simulated.
256 devices in a mesh: dp: 8 (over z), seq: 32 (over x, y, core).
Axes of the slice: x: 4, y: 4, z: 8, core: 2. Of those that a mesh axis runs over, the one named last changes fastest.
Arguments:
- tokens: bfloat16 [8, 16384, 256], P('dp', 'seq'), may hold values from -6 to 6
- cotangent: bfloat16 [8, 16384, 256], P('dp', 'seq'), may hold values from -6 to 6
- w_in: bfloat16 [256, 768], replicated, may hold values from -0.375 to 0.375
- w_out: bfloat16 [256, 256], replicated, may hold values from -0.375 to 0.375
- filter_taps: float32 [16384, 256], P('seq'), may hold values from -0.046875 to 0.046875
- skip: float32 [256], replicated, may hold values from -4 to 4
Outputs:
- output: bfloat16 [8, 16384, 256], P('dp', 'seq')
- dinput: bfloat16 [8, 16384, 256], P('dp', 'seq')
- grad_in_proj: float32 [256, 768], P('dp')
- grad_out_proj: float32 [256, 256], P('dp')
- grad_filter: float32 [16384, 256], P('seq', 'dp')
- grad_skip: float32 [256], P('dp')
All inputs are finite; a program needn't handle non-finite values.
Results may differ from a plain program's by a relative error of at most 0.0049.
Values sent between devices are 32-bit elements; how exact they have to be, the bound alone decides.
A program may use at most 128 MiB of HBM per device.

v0:
```python
import math

import jax
import jax.numpy as jnp
from jax import lax
from jax.sharding import PartitionSpec as P

HIGHEST = lax.Precision.HIGHEST


def regroup_real(signal):
    return lax.all_to_all(signal, "seq", split_axis=1, concat_axis=0, tiled=True)


def regroup_spectral(signal):
    return lax.all_to_all(signal, "seq", split_axis=1, concat_axis=0, tiled=True)


def angles(first_index, second_index, modulus):
    product = first_index[:, None] * second_index[None, :] % modulus
    return 2.0 * math.pi / modulus * product.astype(jnp.float32)


def forward_spectrum(signal):
    tok_rows, chan_count = signal.shape
    seq_parts = lax.axis_size("seq")
    block_rows = tok_rows // seq_parts
    full_length = 2 * seq_parts * tok_rows
    seq_index = lax.axis_index("seq")
    regrouped = regroup_real(signal[None])
    freq_index = jnp.arange(2 * seq_parts, dtype=jnp.int32)
    slot_index = jnp.arange(seq_parts, dtype=jnp.int32)
    outer_angle = angles(freq_index, slot_index, 2 * seq_parts)
    first_re = jnp.einsum("ks,scf->ckf", jnp.cos(outer_angle), regrouped, precision=HIGHEST)
    first_im = jnp.einsum("ks,scf->ckf", -jnp.sin(outer_angle), regrouped, precision=HIGHEST)
    local_pos = seq_index * block_rows + jnp.arange(block_rows, dtype=jnp.int32)
    twiddle = angles(local_pos, freq_index, full_length)[:, :, None]
    tw_cos = jnp.cos(twiddle)
    tw_sin = -jnp.sin(twiddle)
    packed = jnp.concatenate(
        [first_re * tw_cos - first_im * tw_sin, first_re * tw_sin + first_im * tw_cos], axis=2
    )
    spread = regroup_spectral(packed)
    row_index = jnp.arange(tok_rows, dtype=jnp.int32)
    inner_angle = angles(row_index, row_index, tok_rows)
    cos_part = jnp.einsum("kc,cjf->kjf", jnp.cos(inner_angle), spread, precision=HIGHEST)
    sin_part = jnp.einsum("kc,cjf->kjf", -jnp.sin(inner_angle), spread, precision=HIGHEST)
    spectrum = jnp.concatenate(
        [
            cos_part[..., :chan_count] - sin_part[..., chan_count:],
            sin_part[..., :chan_count] + cos_part[..., chan_count:],
        ],
        axis=2,
    )
    spectrum = lax.all_to_all(spectrum, "seq", split_axis=0, concat_axis=1, tiled=True)
    return spectrum


def inverse_field(spectrum):
    spectrum = lax.all_to_all(spectrum, "seq", split_axis=1, concat_axis=0, tiled=True)
    tok_rows = spectrum.shape[0]
    chan_count = spectrum.shape[2] // 2
    seq_parts = lax.axis_size("seq")
    block_rows = tok_rows // seq_parts
    full_length = 2 * seq_parts * tok_rows
    seq_index = lax.axis_index("seq")
    row_index = jnp.arange(tok_rows, dtype=jnp.int32)
    inner_angle = angles(row_index, row_index, tok_rows)
    cos_part = jnp.einsum("kc,kjf->jcf", jnp.cos(inner_angle), spectrum, precision=HIGHEST)
    sin_part = jnp.einsum("kc,kjf->jcf", jnp.sin(inner_angle), spectrum, precision=HIGHEST)
    packed = jnp.concatenate(
        [
            cos_part[..., :chan_count] - sin_part[..., chan_count:],
            sin_part[..., :chan_count] + cos_part[..., chan_count:],
        ],
        axis=2,
    )
    regrouped = regroup_spectral(packed)
    freq_index = jnp.arange(2 * seq_parts, dtype=jnp.int32)
    slot_index = jnp.arange(seq_parts, dtype=jnp.int32)
    local_pos = seq_index * block_rows + jnp.arange(block_rows, dtype=jnp.int32)
    twiddle = angles(freq_index, local_pos, full_length)[:, :, None]
    tw_cos = jnp.cos(twiddle)
    tw_sin = jnp.sin(twiddle)
    moved_re = regrouped[..., :chan_count]
    moved_im = regrouped[..., chan_count:]
    turned_re = moved_re * tw_cos - moved_im * tw_sin
    turned_im = moved_re * tw_sin + moved_im * tw_cos
    outer_angle = angles(slot_index, freq_index, 2 * seq_parts)
    outer_cos = jnp.cos(outer_angle)
    outer_sin = jnp.sin(outer_angle)
    signal = jnp.einsum("sk,kcf->csf", outer_cos, turned_re, precision=HIGHEST) - jnp.einsum(
        "sk,kcf->csf", outer_sin, turned_im, precision=HIGHEST
    )
    signal = signal * (1.0 / full_length)
    return regroup_real(signal)[:, 0, :]


def invert_real(real_part, imag_part):
    return inverse_field(jnp.concatenate([real_part, imag_part], axis=2))


def shards(tokens, cotangent, w_in, w_out, filter_taps, skip):
    model_width = w_out.shape[0]
    seq_in = tokens[0]
    grad_out = cotangent[0]
    projected = jnp.dot(seq_in, w_in, preferred_element_type=jnp.float32)
    gate_out = projected[:, :model_width]
    gate_in = projected[:, model_width : 2 * model_width]
    values = projected[:, 2 * model_width :]
    gated = values * gate_in
    joint_spec = forward_spectrum(jnp.concatenate([gated, filter_taps], axis=1))
    gated_re = joint_spec[..., :model_width]
    taps_re = joint_spec[..., model_width : 2 * model_width]
    gated_im = joint_spec[..., 2 * model_width : 3 * model_width]
    taps_im = joint_spec[..., 3 * model_width :]
    prod_re = taps_re * gated_re - taps_im * gated_im
    prod_im = taps_re * gated_im + taps_im * gated_re
    conv = invert_real(prod_re, prod_im) + skip * gated
    mixed = (conv * gate_out).astype(jnp.bfloat16)
    output = jnp.dot(mixed, w_out, preferred_element_type=jnp.float32).astype(jnp.bfloat16)
    dmixed = lax.dot_general(
        grad_out, w_out, (((1,), (1,)), ((), ())), preferred_element_type=jnp.float32
    )
    dconv = dmixed * gate_out
    dconv_spec = forward_spectrum(dconv)
    dconv_re = dconv_spec[..., :model_width]
    dconv_im = dconv_spec[..., model_width:]
    taps_corr_re = taps_re * dconv_re + taps_im * dconv_im
    taps_corr_im = taps_re * dconv_im - taps_im * dconv_re
    gated_corr_re = gated_re * dconv_re + gated_im * dconv_im
    gated_corr_im = gated_re * dconv_im - gated_im * dconv_re
    back_field = invert_real(
        jnp.concatenate([taps_corr_re, gated_corr_re], axis=2),
        jnp.concatenate([taps_corr_im, gated_corr_im], axis=2),
    )
    dgated = back_field[:, :model_width] + skip * dconv
    taps_term = back_field[:, model_width:]
    dproj = jnp.concatenate([dmixed * conv, dgated * values, dgated * gate_in], axis=1).astype(
        jnp.bfloat16
    )
    dinput = lax.dot_general(
        dproj, w_in, (((1,), (1,)), ((), ())), preferred_element_type=jnp.float32
    ).astype(jnp.bfloat16)
    token_total = lax.axis_size("dp") * tokens.shape[0] * lax.axis_size("seq") * tokens.shape[1]
    grad_scale = 1.0 / math.sqrt(token_total)
    in_term = (
        lax.dot_general(seq_in, dproj, (((0,), (0,)), ((), ())), preferred_element_type=jnp.float32)
        * grad_scale
    )
    out_term = (
        lax.dot_general(
            mixed, grad_out, (((0,), (0,)), ((), ())), preferred_element_type=jnp.float32
        )
        * grad_scale
    )
    skip_term = jnp.sum(dconv * gated, axis=0) * grad_scale
    taps_term = taps_term * grad_scale
    in_sum, out_sum, skip_sum = lax.psum((in_term, out_term, skip_term), "seq")
    in_part, out_part, skip_part, taps_part = (
        lax.psum_scatter(in_sum, "dp", scatter_dimension=0, tiled=True),
        lax.psum_scatter(out_sum, "dp", scatter_dimension=0, tiled=True),
        lax.psum_scatter(skip_sum, "dp", scatter_dimension=0, tiled=True),
        lax.psum_scatter(taps_term, "dp", scatter_dimension=1, tiled=True),
    )
    return (output[None], dinput[None], in_part, out_part, taps_part, skip_part)


def solution(mesh):
    return jax.shard_map(
        shards,
        mesh=mesh,
        in_specs=(P("dp", "seq", None), P("dp", "seq", None), P(), P(), P("seq", None), P()),
        out_specs=(
            P("dp", "seq", None),
            P("dp", "seq", None),
            P("dp", None),
            P("dp", None),
            P("seq", "dp"),
            P("dp"),
        ),
        check_vma=False,
    )
```

profile of v0, /device:TPU:1, one launch (start us, length us, event | category | flops | bytes accessed | tf_op | source)
XLA Modules:
  0.0 731.5 jit_solution(1351603968979599347)
XLA Ops:
  9.5 1.6 multiply_reduce_fusion
  11.3 2.1 copy.107
  13.4 8.6 %all-to-all-start = ((f32[1,512,512]{2,0,1:T(1,128)}), f32[1,512,512]{2,0,1:T(1,128)}, u32[]{:S(2)}, u32[]{:S(2)}) async-start(f32[1,512,512]{2,0,1:T(1,128)} %copy.107), calls=%async_computation | async-start | bytes 2097152 | tf_op jit(solution)/shard_map/all_to_all | solution.py:12
  23.5 15.5 %all-to-all-done = f32[1,512,512]{2,0,1:T(1,128)} async-done(((f32[1,512,512]{2,0,1:T(1,128)}), f32[1,512,512]{2,0,1:T(1,128)}, u32[]{:S(2)}, u32[]{:S(2)}) %all-to-all-start) | async-done | bytes 1048608 | tf_op jit(solution)/shard_map/all_to_all | solution.py:12
  39.0 4.0 all-to-all-start.6
  44.2 2.6 fusion.39
  46.8 3.3 subtract_bitcast_fusion
  50.5 4.5 copy.110
  55.0 7.4 %all-to-all-start.1 = ((f32[16,64,1024]{2,0,1:T(8,128)}), f32[16,64,1024]{2,0,1:T(8,128)}, u32[]{:S(2)}, u32[]{:S(2)}) async-start(f32[16,64,1024]{2,0,1:T(8,128)} %copy.110), calls=%async_computation.1 | async-start | bytes 8388608 | tf_op jit(solution)/shard_map/all_to_all | solution.py:16
  63.8 1.7 subtract_bitcast_fusion.1
  65.8 2.6 copy.127
  68.5 46.2 %all-to-all-done.1 = f32[16,64,1024]{2,0,1:T(8,128)} async-done(((f32[16,64,1024]{2,0,1:T(8,128)}), f32[16,64,1024]{2,0,1:T(8,128)}, u32[]{:S(2)}, u32[]{:S(2)}) %all-to-all-start.1) | async-done | bytes 4194336 | tf_op jit(solution)/shard_map/all_to_all | solution.py:16
  114.7 7.2 all-to-all-start.7
  121.8 2.5 copy.111
  124.3 10.9 %fusion.25 = f32[512,2,1024]{2,0,1:T(8,128)S(1)} fusion(f32[512,2,1024]{2,0,1:T(8,128)S(1)} %bitcast.153), kind=kOutput, calls=%fused_computation.52 | convolution fusion | flops 6446383104 | bytes 8388608 | tf_op jit(solution)/shard_map/kc,cjf->kjf/dot_general | solution.py:47
  135.2 19.6 %fusion.31 = f32[512,2,1024]{2,0,1:T(8,128)S(1)} fusion(f32[512,2,1024]{2,0,1:T(8,128)S(1)} %bitcast.154), kind=kOutput, calls=%fused_computation.58 | convolution fusion | flops 6446120960 | bytes 8388608 | tf_op jit(solution)/shard_map/kc,cjf->kjf/dot_general | solution.py:46
  156.3 5.7 copy.112
  161.9 7.4 %all-to-all-start.2 = ((f32[512,2,1024]{2,1,0:T(2,128)}), f32[512,2,1024]{2,1,0:T(2,128)}, u32[]{:S(2)}, u32[]{:S(2)}) async-start(f32[512,2,1024]{2,1,0:T(2,128)} %copy.112), calls=%async_computation.2 | async-start | bytes 8388608 | tf_op jit(solution)/shard_map/all_to_all | solution.py:55
  169.4 1.8 copy.128
  171.2 10.7 %fusion.23 = f32[512,2,512]{0,2,1:T(8,128)S(1)} fusion(f32[512,2,512]{2,0,1:T(8,128)S(1)} %bitcast.170), kind=kOutput, calls=%fused_computation.50 | convolution fusion | flops 3225157632 | bytes 4194304 | tf_op jit(solution)/shard_map/kc,cjf->kjf/dot_general | solution.py:47
  181.9 10.6 %fusion.28 = f32[512,2,512]{0,2,1:T(8,128)S(1)} fusion(f32[512,2,512]{2,0,1:T(8,128)S(1)} %bitcast.171), kind=kOutput, calls=%fused_computation.55 | convolution fusion | flops 3224895488 | bytes 4194304 | tf_op jit(solution)/shard_map/kc,cjf->kjf/dot_general | solution.py:46
  193.0 1.6 pad_maximum_fusion.7
  194.6 4.1 copy.131
  198.7 22.9 %all-to-all-done.2 = f32[512,2,1024]{2,1,0:T(2,128)} async-done(((f32[512,2,1024]{2,1,0:T(2,128)}), f32[512,2,1024]{2,1,0:T(2,128)}, u32[]{:S(2)}, u32[]{:S(2)}) %all-to-all-start.2) | async-done | bytes 4194336 | tf_op jit(solution)/shard_map/all_to_all | solution.py:55
  221.6 7.2 all-to-all-start.8
  228.8 3.5 copy.113
  233.2 1.6 copy-done.1
  234.9 1.7 pad_maximum_fusion.4
  236.6 20.5 %all-to-all-done.8 = f32[512,2,512]{2,1,0:T(2,128)} async-done(((f32[512,2,512]{2,1,0:T(2,128)}), f32[512,2,512]{2,1,0:T(2,128)}, u32[]{:S(2)}, u32[]{:S(2)}) %all-to-all-start.8) | async-done | bytes 2097184 | tf_op jit(solution)/shard_map/all_to_all | solution.py:55
  257.1 5.2 all-to-all-start.3
  262.3 2.0 copy.132
  264.5 2.0 copy-done.2
  267.1 2.7 pad_maximum_fusion.2
  269.8 21.0 %all-to-all-done.3 = f32[16,64,512]{2,0,1:T(8,128)} async-done(((f32[16,64,512]{2,0,1:T(8,128)}), f32[16,64,512]{2,0,1:T(8,128)}, u32[]{:S(2)}, u32[]{:S(2)}) %all-to-all-start.3) | async-done | bytes 2097184 | tf_op jit(solution)/shard_map/all_to_all | solution.py:60
  290.8 5.3 all-to-all-start.9
  296.1 1.8 copy.115
  297.9 11.0 %convolution_bitcast_fusion.2 = f32[2,512,512]{1,2,0:T(8,128)S(1)} fusion(f32[512,2,512]{2,0,1:T(8,128)S(1)} %bitcast.172), kind=kOutput, calls=%fused_computation.22 | convolution fusion | flops 3224895488 | bytes 4194304 | tf_op jit(solution)/shard_map/kc,kjf->jcf/dot_general | solution.py:70
  308.9 11.0 %convolution_bitcast_fusion.3 = f32[2,512,512]{1,2,0:T(8,128)S(1)} fusion(f32[512,2,512]{2,0,1:T(8,128)S(1)} %bitcast.173), kind=kOutput, calls=%fused_computation.23 | convolution fusion | flops 3224895488 | bytes 4194304 | tf_op jit(solution)/shard_map/kc,kjf->jcf/dot_general | solution.py:69
  320.4 1.6 pad_maximum_fusion.5
  322.0 4.1 copy.118
  326.1 22.2 %all-to-all-done.9 = f32[16,64,1024]{2,0,1:T(8,128)} async-done(((f32[16,64,1024]{2,0,1:T(8,128)}), f32[16,64,1024]{2,0,1:T(8,128)}, u32[]{:S(2)}, u32[]{:S(2)}) %all-to-all-start.9) | async-done | bytes 4194336 | tf_op jit(solution)/shard_map/all_to_all | solution.py:60
  348.4 7.6 %all-to-all-start.4 = ((f32[2,512,512]{2,0,1:T(2,128)}), f32[2,512,512]{2,0,1:T(2,128)}, u32[]{:S(2)}, u32[]{:S(2)}) async-start(f32[2,512,512]{2,0,1:T(2,128)} %copy.118), calls=%async_computation.4 | async-start | bytes 4194304 | tf_op jit(solution)/shard_map/all_to_all | solution.py:16
  356.0 2.5 copy.134
  358.5 11.1 %convolution_bitcast_fusion = f32[2,512,1024]{1,2,0:T(8,128)S(1)} fusion(f32[512,2,1024]{2,0,1:T(8,128)S(1)} %bitcast.155), kind=kOutput, calls=%fused_computation.4 | convolution fusion | flops 6446120960 | bytes 8388608 | tf_op jit(solution)/shard_map/kc,kjf->jcf/dot_general | solution.py:70
  369.6 11.3 %convolution_bitcast_fusion.1 = f32[2,512,1024]{1,2,0:T(8,128)S(1)} fusion(f32[512,2,1024]{2,0,1:T(8,128)S(1)} %bitcast.156), kind=kOutput, calls=%fused_computation.5 | convolution fusion | flops 6446120960 | bytes 8388608 | tf_op jit(solution)/shard_map/kc,kjf->jcf/dot_general | solution.py:69
  381.9 2.5 pad_maximum_fusion.3
  384.4 7.4 %copy.137 = f32[2,512,1024]{2,0,1:T(2,128)} copy(f32[2,512,1024]{1,2,0:T(8,128)} %pad_maximum_fusion.3) | data formatting | bytes 8388608 | tf_op jit(solution)/shard_map/concatenate | solution.py:71
  391.7 7.6 %all-to-all-start.10 = ((f32[2,512,1024]{2,0,1:T(2,128)}), f32[2,512,1024]{2,0,1:T(2,128)}, u32[]{:S(2)}, u32[]{:S(2)}) async-start(f32[2,512,1024]{2,0,1:T(2,128)} %copy.137), calls=%async_computation.10 | async-start | bytes 8388608 | tf_op jit(solution)/shard_map/all_to_all | solution.py:16
  399.5 2.0 copy.119
  406.0 45.5 %all-to-all-done.10 = f32[2,512,1024]{2,0,1:T(2,128)} async-done(((f32[2,512,1024]{2,0,1:T(2,128)}), f32[2,512,1024]{2,0,1:T(2,128)}, u32[]{:S(2)}, u32[]{:S(2)}) %all-to-all-start.10) | async-done | bytes 4194336 | tf_op jit(solution)/shard_map/all_to_all | solution.py:16
  451.6 7.1 all-to-all-start.5
  458.7 3.5 copy.138
  463.6 2.5 fusion
  466.1 2.6 fusion.10
  468.8 1.6 copy.142
  470.4 24.4 %all_to_all.198 = f32[16,32,512]{2,0,1:T(8,128)S(1)} all-to-all(f32[16,32,512]{2,0,1:T(8,128)} %copy.142), channel_id=1, replica_groups=mesh['dp'=8,'seq'=32] {'seq'}, dimensions={1} | all-to-all | bytes 2097152 | tf_op jit(solution)/shard_map/all_to_all | solution.py:12
  494.8 2.4 multiply_convert_fusion.1
  500.7 31.2 %reduce-scatter.12.cloned.1.call-done = f32[32,768]{1,0:T(8,128)} async-done(((f32[256,768]{1,0:T(8,128)}), f32[32,768]{1,0:T(8,128)}) %reduce-scatter.12.cloned.1.call-update) | async-done | bytes 98320
  532.0 1.8 copy.154
  536.1 12.0 %all-reduce = f32[256]{0:T(256)S(1)} all-reduce(f32[256]{0:T(256)S(1)} %broadcast_multiply_fusion), channel_id=5, replica_groups=mesh['dp'=8,'seq'=32] {'dp'}, use_global_device_ids=true, to_apply=%region_7.8.clone | all-reduce | flops 256 | bytes 2048
  550.2 19.2 %reduce-scatter.8.cloned.1.call-done = f32[32,256]{1,0:T(8,128)} async-done(((f32[256,256]{1,0:T(8,128)}), f32[32,256]{1,0:T(8,128)}) %reduce-scatter.8.cloned.1.call-update) | async-done | bytes 32784 | tf_op jit(solution)/shard_map/reduce_scatter | solution.py:162
  569.4 124.4 %all-reduce.1 = (f32[32,256]{1,0:T(8,128)}, f32[32]{0:T(128)}) all-reduce(f32[32,256]{1,0:T(8,128)} %reduce-scatter.8.cloned.1.call-done, f32[32]{0:T(128)S(1)} %dynamic-slice.1), channel_id=1, replica_groups=mesh['dp'=8,'seq'=32] {'seq'}, use_global_device_ids=true, to_apply=%region_2.3 | all-reduce | flops 8224 | bytes 65792 | tf_op jit(solution)/shard_map/psum | solution.py:159
  693.8 1.8 copy.143
  695.6 29.1 %reduce-scatter.10.cloned.1.call-done = f32[32,512]{1,0:T(8,128)} async-done(((f32[256,512]{1,0:T(8,128)}), f32[32,512]{1,0:T(8,128)}) %reduce-scatter.10.cloned.1.call-update) | async-done | bytes 65552
  (97 shorter events, 25.6 us)
Async XLA Ops:
  7.2 1.0 copy-start
  7.2 2.3 copy-start.6
  7.2 2.3 copy-start.8
  7.2 3.9 copy-start.10
  13.4 25.6 %all-to-all-start = ((f32[1,512,512]{2,0,1:T(1,128)}), f32[1,512,512]{2,0,1:T(1,128)}, u32[]{:S(2)}, u32[]{:S(2)}) async-start(f32[1,512,512]{2,0,1:T(1,128)} %copy.107), calls=%async_computation | async-start | bytes 2097152 | tf_op jit(solution)/shard_map/all_to_all | solution.py:12
  23.4 15.6 %copy-start.21 = (s32[16]{0:T(128)}, s32[16]{0:T(128)S(1)}, u32[]{:S(2)}) copy-start(s32[16]{0:T(128)S(1)} %iota_add_fusion) | copy-start | bytes 196
  39.0 16.0 %all-to-all-start.6 = ((f32[1,512,256]{2,0,1:T(1,128)}), f32[1,512,256]{2,0,1:T(1,128)S(1)}, u32[]{:S(2)}, u32[]{:S(2)}) async-start(f32[1,512,256]{2,0,1:T(1,128)} %copy.124), calls=%async_computation.6 | async-start | bytes 1048576 | tf_op jit(solution)/shard_map/all_to_all | solution.py:12
  55.0 59.7 %all-to-all-start.1 = ((f32[16,64,1024]{2,0,1:T(8,128)}), f32[16,64,1024]{2,0,1:T(8,128)}, u32[]{:S(2)}, u32[]{:S(2)}) async-start(f32[16,64,1024]{2,0,1:T(8,128)} %copy.110), calls=%async_computation.1 | async-start | bytes 8388608 | tf_op jit(solution)/shard_map/all_to_all | solution.py:16
  114.7 47.3 %all-to-all-start.7 = ((f32[16,64,512]{2,0,1:T(8,128)}), f32[16,64,512]{2,0,1:T(8,128)}, u32[]{:S(2)}, u32[]{:S(2)}) async-start(f32[16,64,512]{2,0,1:T(8,128)} %copy.127), calls=%async_computation.7 | async-start | bytes 4194304 | tf_op jit(solution)/shard_map/all_to_all | solution.py:16
  161.9 59.7 %all-to-all-start.2 = ((f32[512,2,1024]{2,1,0:T(2,128)}), f32[512,2,1024]{2,1,0:T(2,128)}, u32[]{:S(2)}, u32[]{:S(2)}) async-start(f32[512,2,1024]{2,1,0:T(2,128)} %copy.112), calls=%async_computation.2 | async-start | bytes 8388608 | tf_op jit(solution)/shard_map/all_to_all | solution.py:55
  221.6 35.5 %all-to-all-start.8 = ((f32[512,2,512]{2,1,0:T(2,128)}), f32[512,2,512]{2,1,0:T(2,128)}, u32[]{:S(2)}, u32[]{:S(2)}) async-start(f32[512,2,512]{2,1,0:T(2,128)} %copy.131), calls=%async_computation.8 | async-start | bytes 4194304 | tf_op jit(solution)/shard_map/all_to_all | solution.py:55
  232.9 2.0 copy-start.1
  257.1 33.6 %all-to-all-start.3 = ((f32[16,64,512]{2,0,1:T(8,128)}), f32[16,64,512]{2,0,1:T(8,128)}, u32[]{:S(2)}, u32[]{:S(2)}) async-start(f32[16,64,512]{2,0,1:T(8,128)} %pad_maximum_fusion.4), calls=%async_computation.3 | async-start | bytes 4194304 | tf_op jit(solution)/shard_map/all_to_all | solution.py:60
  264.3 2.2 copy-start.2
  290.8 57.6 %all-to-all-start.9 = ((f32[16,64,1024]{2,0,1:T(8,128)}), f32[16,64,1024]{2,0,1:T(8,128)}, u32[]{:S(2)}, u32[]{:S(2)}) async-start(f32[16,64,1024]{2,0,1:T(8,128)} %pad_maximum_fusion.2), calls=%async_computation.9 | async-start | bytes 8388608 | tf_op jit(solution)/shard_map/all_to_all | solution.py:60
  348.4 43.4 %all-to-all-start.4 = ((f32[2,512,512]{2,0,1:T(2,128)}), f32[2,512,512]{2,0,1:T(2,128)}, u32[]{:S(2)}, u32[]{:S(2)}) async-start(f32[2,512,512]{2,0,1:T(2,128)} %copy.118), calls=%async_computation.4 | async-start | bytes 4194304 | tf_op jit(solution)/shard_map/all_to_all | solution.py:16
  391.7 7.6 %copy-start.22 = (s32[16]{0:T(128)S(1)}, s32[16]{0:T(128)}, u32[]{:S(2)}) copy-start(s32[16]{0:T(128)} %copy-done.21) | copy-start | bytes 196
  391.7 59.8 %all-to-all-start.10 = ((f32[2,512,1024]{2,0,1:T(2,128)}), f32[2,512,1024]{2,0,1:T(2,128)}, u32[]{:S(2)}, u32[]{:S(2)}) async-start(f32[2,512,1024]{2,0,1:T(2,128)} %copy.137), calls=%async_computation.10 | async-start | bytes 8388608 | tf_op jit(solution)/shard_map/all_to_all | solution.py:16
  399.5 2.3 copy-start.11
  399.5 2.3 copy-start.13
  451.6 18.8 %all-to-all-start.5 = ((f32[16,32,256]{2,0,1:T(8,128)}), f32[16,32,256]{2,0,1:T(8,128)S(1)}, u32[]{:S(2)}, u32[]{:S(2)}) async-start(f32[16,32,256]{2,0,1:T(8,128)} %copy.123), calls=%async_computation.5 | async-start | bytes 1048576 | tf_op jit(solution)/shard_map/all_to_all | solution.py:12
  458.7 73.3 %reduce-scatter.12.cloned.1.call-start = ((), (), s32[]{:S(2)}) async-start(), calls=%async_computation.18 | async-start | bytes 884736
  462.3 0.8 copy-start.12
  462.3 0.8 copy-start.14
  468.7 26.1 %copy-start.23 = (f32[256]{0:T(256)S(1)}, f32[256]{0:T(256)}, u32[]{:S(2)}) copy-start(f32[256]{0:T(256)} %param.11) | copy-start | bytes 3076
  470.4 24.4 %copy-start.4 = (f32[16,32,256]{2,0,1:T(8,128)}, f32[16,32,256]{2,0,1:T(8,128)S(1)}, u32[]{:S(2)}) copy-start(f32[16,32,256]{2,0,1:T(8,128)S(1)} %all-to-all-done.5) | copy-start | bytes 1572868
  470.4 24.4 %copy-start.5 = (f32[512,256]{1,0:T(8,128)S(1)}, f32[512,256]{1,0:T(8,128)}, u32[]{:S(2)}) copy-start(f32[512,256]{1,0:T(8,128)} %get-tuple-element.72) | copy-start | bytes 1572868
  494.8 3.2 copy-start.15
  497.2 0.7 copy-start.16
  497.2 0.8 copy-start.18
  498.0 1.7 copy-start.7
  498.4 35.4 %copy-start.3 = (f32[512,256]{1,0:T(8,128)S(1)}, f32[512,256]{1,0:T(8,128)}, u32[]{:S(2)}) copy-start(f32[512,256]{1,0:T(8,128)} %get-tuple-element.67) | copy-start | bytes 1572868
  499.6 35.3 %copy-start.24 = (u32[256]{0:T(256)S(1)}, u32[256]{0:T(256)}, u32[]{:S(2)}) copy-start(u32[256]{0:T(256)} %constant.108) | copy-start | bytes 3076
  499.6 36.5 %copy-start.20 = (f32[256]{0:T(256)S(1)}, f32[256]{0:T(256)}, u32[]{:S(2)}) copy-start(f32[256]{0:T(256)} %get-tuple-element.38) | copy-start | bytes 3076
  499.6 48.6 %copy-start.9 = (bf16[256,256]{1,0:T(8,128)(2,1)S(1)}, bf16[256,256]{1,0:T(8,128)(2,1)}, u32[]{:S(2)}) copy-start(bf16[256,256]{1,0:T(8,128)(2,1)} %param.9) | copy-start | bytes 393220
  499.6 69.8 %reduce-scatter.8.cloned.1.call-start = ((), (), s32[]{:S(2)}) async-start(), calls=%async_computation.16 | async-start | bytes 294912 | tf_op jit(solution)/shard_map/reduce_scatter | solution.py:162
  499.7 49.4 %copy-start.17 = (bf16[512,256]{1,0:T(8,128)(2,1)S(1)}, bf16[512,256]{1,0:T(8,128)(2,1)}, u32[]{:S(2)}) copy-start(bf16[512,256]{1,0:T(8,128)(2,1)} %copy-done.16) | copy-start | bytes 786436
  499.7 49.4 %copy-start.19 = (bf16[512,256]{1,0:T(8,128)(2,1)S(1)}, bf16[512,256]{1,0:T(8,128)(2,1)}, u32[]{:S(2)}) copy-start(bf16[512,256]{1,0:T(8,128)(2,1)} %copy-done.18) | copy-start | bytes 786436
  500.7 193.1 %all-reduce.4.cloned.1.call-start = ((), (), s32[]{:S(2)}) async-start(), calls=%async_computation.15 | async-start | bytes 786432 | tf_op jit(solution)/shard_map/psum | solution.py:159
  533.8 190.9 %reduce-scatter.10.cloned.1.call-start = ((), (), s32[]{:S(2)}) async-start(), calls=%async_computation.17 | async-start | bytes 589824
Sparse Core Ops, SparseCore 0:
  499.7 32.1 reduce-scatter.11
  534.6 34.7 reduce-scatter.7
  572.6 116.8 all-reduce.3
  692.4 32.1 reduce-scatter.9
where the time goes:
time: 746 us; the launch traced here: 732 us
  waiting for transfers between devices  273 us (37%)
  blocking collectives  161 us (22%)
  matrix products  119 us (16%)
  starting transfers between devices  74.8 us (10%)
  local copies, waits for them, and re-layouts  69.3 us (9%)
  other arithmetic  18.7 us (3%)
  between operations  15.4 us (2%)
    psum x1, blocking collectives, shards(): in_sum, out_sum, skip_sum = lax.psum((in_term, out_term, skip_term), 'seq')  124 us
    all_to_all x4, waiting for transfers between devices, regroup_spectral(): lax.all_to_all(signal, 'seq', split_axis=1, concat_axis=0, tiled=True)  91.7 us
    unnamed x6, waiting for transfers between devices  60.4 us
    all_to_all x2, waiting for transfers between devices, forward_spectrum(): lax.all_to_all(spectrum, 'seq', split_axis=0, concat_axis=1, tiled=True)  43.4 us
    all_to_all x2, waiting for transfers between devices, inverse_field(): lax.all_to_all(spectrum, 'seq', split_axis=1, concat_axis=0, tiled=True)  43.2 us
    dot_general x2, matrix products, forward_spectrum(): jnp.einsum('kc,cjf->kjf', jnp.cos(inner_angle), spread, precision=HIGHEST)  30.2 us
    all_to_all x4, starting transfers between devices, regroup_spectral(): lax.all_to_all(signal, 'seq', split_axis=1, concat_axis=0, tiled=True)  29.8 us
    all_to_all x1, blocking collectives, regroup_real(): lax.all_to_all(signal, 'seq', split_axis=1, concat_axis=0, tiled=True)  24.4 us
  transfers between devices with their start and end apart: 15, of which 10 were waited for; matrix products, arithmetic and copies ran while one was open for 26% of the time, Pallas kernels for 0%

commit v1 on v0

v1 whole, which is shorter than its diff:
```python
import functools
import math

import jax
import jax.numpy as jnp
import numpy as np
from jax import lax
from jax.experimental import pallas as pl
from jax.experimental.pallas import tpu as pltpu
from jax.sharding import PartitionSpec as P

F32 = jnp.float32
BF16 = jnp.bfloat16
ROWS = 16
NT = (((1,), (1,)), ((), ()))
TN = (((0,), (0,)), ((), ()))


def tables(block):
    def turn(numer):
        angle = np.pi / (2 * block) * (numer % (4 * block))
        return np.cos(angle), np.sin(angle)

    pos = np.arange(block)
    coarse = np.arange(block // ROWS) * ROWS
    fine = np.arange(ROWS)
    odd = 2 * pos + 1
    parts = [
        *turn(np.outer(coarse, odd)),
        *turn(np.outer(fine, odd)),
        *turn(np.outer(2 * coarse, pos)),
        *turn(np.outer(2 * fine + 1, pos)),
    ]
    return np.concatenate(parts, axis=0).astype(np.float32)


def split2(x):
    high = x.astype(BF16)
    return high, (x - high.astype(F32)).astype(BF16)


def split3(x):
    high = x.astype(BF16)
    rest = x - high.astype(F32)
    mid = rest.astype(BF16)
    return high, mid, (rest - mid.astype(F32)).astype(BF16)


def dot(a, b, dims=(((1,), (0,)), ((), ()))):
    return lax.dot_general(a, b, dims, preferred_element_type=F32)


def block_conv(p_ref, q_ref, o_ref, block, size, corr):
    count = q_ref.shape[0]
    groups = count // size
    lanes = min(128, block)

    def tile(t, _):
        re = pl.ds(pl.multiple_of(t * lanes, lanes), lanes)
        im = pl.ds(pl.multiple_of(block + t * lanes, lanes), lanes)

        def chunk(acc, out0, in0, diag):
            acc = list(acc)
            cache = {}
            base = in0 - out0 if corr else out0 - in0
            for u in range(size):
                qr, qi = q_ref[in0 + u, :, re], q_ref[in0 + u, :, im]
                for r in range(size):
                    lag = u - r if corr else r - u
                    if diag and lag < 0:
                        continue
                    if lag not in cache:
                        cache[lag] = p_ref[base + lag, :, re], p_ref[base + lag, :, im]
                    pr, pi = cache[lag]
                    if corr:
                        new_re, new_im = pr * qr + pi * qi, pr * qi - pi * qr
                    else:
                        new_re, new_im = pr * qr - pi * qi, pr * qi + pi * qr
                    acc[2 * r] = acc[2 * r] + new_re
                    acc[2 * r + 1] = acc[2 * r + 1] + new_im
            return tuple(acc)

        def group(g, _):
            out0 = g * size
            zero = jnp.zeros((q_ref.shape[1], lanes), F32)
            acc = chunk((zero,) * (2 * size), out0, out0, True)

            def step(h, acc):
                return chunk(acc, out0, h * size, False)

            low, top = (g + 1, groups) if corr else (0, g)
            acc = lax.fori_loop(low, top, step, acc)
            for r in range(size):
                o_ref[out0 + r, :, re] = acc[2 * r]
                o_ref[out0 + r, :, im] = acc[2 * r + 1]
            return 0

        lax.fori_loop(0, groups, group, 0)
        return 0

    lax.fori_loop(0, block // lanes, tile, 0)


def body(
    seq_n,
    dp_n,
    scale,
    tok,
    cot,
    w_in,
    w_out,
    taps,
    skip,
    tab,
    out,
    dinp,
    gin,
    gout,
    gfil,
    gskip,
    tap_s,
    gat_s,
    dcn_s,
    tap_r,
    gat_r,
    dcn_r,
    proj,
    dmx,
    w_t,
    w_o,
    tok_t,
    f_mat,
    b_mat,
    h_sp,
    x_sp,
    d_sp,
    o_sp,
    con_s,
    dga_s,
    con_r,
    dga_r,
    gf_t,
    gf_s,
    gf_r,
    sk_s,
    sk_r,
    q_s,
    q_r,
    dproj,
    g1_s,
    g2_s,
    g1_r,
    g2_r,
    z_s,
    z_r,
    a_s,
    a_r,
    send,
    recv,
):
    block, width = tok.shape
    chans = width // seq_n
    me = lax.axis_index("seq")
    my_dp = lax.axis_index("dp")
    group = 8 if seq_n >= 32 else 4

    barrier = pltpu.get_barrier_semaphore()

    def greet_seq(k, _):
        pl.semaphore_signal(barrier, 1, device_id={"seq": lax.rem(me + k, seq_n)})
        return 0

    def greet_dp(k, _):
        pl.semaphore_signal(barrier, 1, device_id={"dp": lax.rem(my_dp + k, dp_n)})
        return 0

    lax.fori_loop(1, seq_n, greet_seq, 0)
    lax.fori_loop(1, dp_n, greet_dp, 0)

    def exchange(src, dst, slot, axis="seq", gather=False):
        mine, parts = (me, seq_n) if axis == "seq" else (my_dp, dp_n)
        own = src if gather else src.at[mine]
        pltpu.make_async_copy(own, dst.at[mine], recv.at[slot]).start()

        def go(k, _):
            peer = lax.rem(mine + k, parts)
            pltpu.make_async_remote_copy(
                src if gather else src.at[peer],
                dst.at[mine],
                send.at[slot],
                recv.at[slot],
                device_id={axis: peer},
            ).start()
            return 0

        lax.fori_loop(1, parts, go, 0)

    def arrived(dst, slot):
        pltpu.make_async_copy(dst, dst, recv.at[slot]).wait()

    def sent(dst, slot):
        rest = dst.at[pl.ds(0, dst.shape[0] - 1)]
        pltpu.make_async_copy(rest, rest, send.at[slot]).wait()

    row = lax.broadcasted_iota(jnp.int32, (width, width), 0)
    col = lax.broadcasted_iota(jnp.int32, (width, width), 1)
    hit = (col % seq_n) * chans + col // seq_n == row
    perm = jnp.where(hit, 1.0, 0.0).astype(BF16)
    skip_col = jnp.sum(jnp.where(hit, skip[...], 0.0), axis=1, keepdims=True)

    high, low = split2(taps[...])
    taps_t = dot(perm, high, NT) + dot(perm, low, NT)
    tap_s[...] = taps_t.reshape(seq_n, chans, block)
    pl.semaphore_wait(barrier, seq_n + dp_n - 2)
    exchange(tap_s, tap_r, 0)

    for part in range(3):
        rows = pl.ds(part * width, width)
        w_t[rows, :] = dot(perm, w_in[:, part * width : (part + 1) * width], NT).astype(BF16)
        proj[rows, :] = dot(w_t[rows, :], tok[...], NT)
    gate_out = proj.at[pl.ds(0, width)]
    gate_in = proj.at[pl.ds(width, width)]
    values = proj.at[pl.ds(2 * width, width)]
    gat_s[...] = (values[...] * gate_in[...]).reshape(seq_n, chans, block)
    exchange(gat_s, gat_r, 1)

    w_o[...] = dot(perm, w_out[...]).astype(BF16)
    dmx[...] = dot(w_o[...], cot[...], NT)
    dcn_s[...] = (dmx[...] * gate_out[...]).reshape(seq_n, chans, block)
    exchange(dcn_s, dcn_r, 2)
    tok_t[...] = dot(perm, tok[...], NT).astype(BF16)

    big = block // ROWS

    def build(dst, first, vertical):
        cos_f = tab[pl.ds(first + 2 * big, ROWS), :]
        sin_f = tab[pl.ds(first + 2 * big + ROWS, ROWS), :]

        def rows_of(a, _):
            cos_c = tab[pl.ds(first + a, 1), :]
            sin_c = tab[pl.ds(first + big + a, 1), :]
            cos = cos_c * cos_f - sin_c * sin_f
            sin = -(sin_c * cos_f + cos_c * sin_f)
            at = pl.multiple_of(a * ROWS, ROWS)
            for k, value in enumerate((cos, sin)):
                high, low = split2(value)
                for copy, piece in enumerate((high, high, low)):
                    if vertical:
                        dst[pl.ds((2 * copy + k) * block + at, ROWS), :] = piece
                    else:
                        dst[pl.ds(copy * block + at, ROWS), k * block : (k + 1) * block] = piece
            return 0

        lax.fori_loop(0, big, rows_of, 0)

    build(f_mat, 0, False)
    build(b_mat, 2 * big + 2 * ROWS, True)

    rows_n = seq_n * chans
    step = min(256, block)

    def spectrum(src, dst):
        high, low = split2(src[...].reshape(rows_n, block))
        wide = jnp.concatenate([high, low, high], axis=1)
        for n in range(0, 2 * block, step):
            dst[:, :, n : n + step] = dot(wide, f_mat[:, n : n + step]).reshape(seq_n, chans, step)

    def field(factor):
        high, low = split2(o_sp[...].reshape(rows_n, 2 * block))
        wide = jnp.concatenate([high, low, high], axis=1)
        return dot(wide, b_mat[...]) * factor

    odd = lax.broadcasted_iota(jnp.int32, (1, 1, block), 2) % 2
    sign = (1 - 2 * odd).astype(F32)

    arrived(tap_r, 0)
    spectrum(tap_r, o_sp)
    h_sp[0] = o_sp[0]
    h_sp[1:, :, :block] = o_sp[1:, :, :block] - sign * o_sp[: seq_n - 1, :, block:]
    h_sp[1:, :, block:] = o_sp[1:, :, block:] + sign * o_sp[: seq_n - 1, :, :block]

    arrived(gat_r, 1)
    spectrum(gat_r, x_sp)
    block_conv(h_sp, x_sp, o_sp, block, group, False)
    con_s[...] = field(1.0 / block).reshape(seq_n, chans, block)
    exchange(con_s, con_r, 3)

    arrived(dcn_r, 2)
    spectrum(dcn_r, d_sp)
    block_conv(h_sp, d_sp, o_sp, block, group, True)
    dga_s[...] = field(1.0 / block).reshape(seq_n, chans, block)
    exchange(dga_s, dga_r, 4)

    block_conv(x_sp, d_sp, h_sp, block, group, True)
    last = seq_n - 1
    o_sp[last] = h_sp[last]
    o_sp[:last, :, :block] = h_sp[:last, :, :block] + sign * h_sp[1:, :, block:]
    o_sp[:last, :, block:] = h_sp[:last, :, block:] - sign * h_sp[1:, :, :block]
    lanes = block // 4
    term = field(scale / block)
    for r in range(4):
        gf_t[r] = term[:, r * lanes : (r + 1) * lanes]
        for d in range(dp_n):
            gf_s[d, :, r * lanes : (r + 1) * lanes] = gf_t[r, pl.ds(d, seq_n, stride=chans), :]
    both = jnp.sum(gat_r[...] * dcn_r[...], axis=0)
    narrow = both[:, :lanes]
    for r in range(1, 4):
        narrow = narrow + both[:, r * lanes : (r + 1) * lanes]
    for d in range(dp_n):
        sk_s[d] = jnp.broadcast_to(narrow[d : d + 1, :], (8, lanes))
    exchange(gf_s, gf_r, 5, "dp")
    exchange(sk_s, sk_r, 6, "dp")

    arrived(con_r, 3)
    gated = gat_s[...].reshape(width, block)
    conv = con_r[...].reshape(width, block) + skip_col * gated
    mixed = (conv * gate_out[...]).astype(BF16)
    dproj[pl.ds(0, width), :] = (dmx[...] * conv).astype(BF16)
    g1_s[:, :, :width] = dot(tok_t[...], dproj[pl.ds(0, width), :], NT).reshape(seq_n, chans, width)
    g1_s[:, :, width:] = dot(mixed, cot[...]).reshape(seq_n, chans, width)
    exchange(g1_s, g1_r, 7)
    out[...] = dot(mixed, w_o[...], TN).astype(BF16)

    arrived(gf_r, 5)
    arrived(sk_r, 6)
    gf_sum = jnp.sum(gf_r[...], axis=0)
    sk_sum = jnp.sum(sk_r[...], axis=0) * scale
    for r in range(4):
        q_s[:, r, :] = gf_sum[:, r * lanes : (r + 1) * lanes]
    q_s[:, 4, :] = jnp.broadcast_to(sk_sum[0:1, :], (seq_n, lanes))
    exchange(q_s, q_r, 8)

    arrived(dga_r, 4)
    dgated = dga_r[...].reshape(width, block) + skip_col * dcn_s[...].reshape(width, block)
    dproj[pl.ds(width, width), :] = (dgated * values[...]).astype(BF16)
    dproj[pl.ds(2 * width, width), :] = (dgated * gate_in[...]).astype(BF16)
    for k in (0, 1):
        term = dot(tok_t[...], dproj[pl.ds((k + 1) * width, width), :], NT)
        g2_s[:, :, k * width : (k + 1) * width] = term.reshape(seq_n, chans, width)
    exchange(g2_s, g2_r, 9)
    dinp[...] = dot(dproj[...], w_t[...], TN).astype(BF16)

    arrived(q_r, 8)
    for r in range(4):
        gfil[r * lanes : (r + 1) * lanes, :] = q_r[:, r, :].T
    gskip[...] = jnp.sum(q_r[:, 4, :].T, axis=0, keepdims=True)

    arrived(g1_r, 7)
    sum1 = jnp.sum(g1_r[...], axis=0) * scale
    arrived(g2_r, 9)
    sum2 = jnp.sum(g2_r[...], axis=0) * scale
    piece = 2 * width // 4
    for r in range(4):
        z_s[:, r, :] = sum1[:, r * piece : (r + 1) * piece]
        z_s[:, 4 + r, :] = sum2[:, r * piece : (r + 1) * piece]
    exchange(z_s, z_r, 10, "dp")
    arrived(z_r, 10)
    a_s[...] = jnp.sum(z_r[...], axis=0)
    exchange(a_s, a_r, 11, gather=True)
    arrived(a_r, 11)

    def line(r):
        return jnp.concatenate([a_r[:, r, :], a_r[:, r + 1, :]], axis=1)

    gout[...] = line(2)
    for k, r in enumerate((0, 4, 6)):
        h, m, t = split3(line(r))
        gin[:, k * width : (k + 1) * width] = dot(h, perm) + (dot(m, perm) + dot(t, perm))

    for slot, ref in enumerate(
        (tap_r, gat_r, dcn_r, con_r, dga_r, gf_r, sk_r, g1_r, q_r, g2_r, z_r, a_r)
    ):
        sent(ref, slot)


def shards(tokens, cotangent, w_in, w_out, filter_taps, skip):
    seq_n, dp_n = lax.axis_size("seq"), lax.axis_size("dp")
    block, width = tokens.shape[1:]
    chans = width // seq_n
    scale = 1.0 / math.sqrt(dp_n * seq_n * block)
    own = width // dp_n

    def shape(*dims, dtype=F32):
        return pltpu.VMEM(dims, dtype)

    ex = (seq_n, chans, block)
    sp = (seq_n, chans, 2 * block)
    scratch = [
        *[shape(*ex)] * 6,
        shape(3 * width, block),
        shape(width, block),
        shape(3 * width, width, dtype=BF16),
        shape(width, width, dtype=BF16),
        shape(width, block, dtype=BF16),
        shape(3 * block, 2 * block, dtype=BF16),
        shape(6 * block, block, dtype=BF16),
        *[shape(*sp)] * 4,
        *[shape(*ex)] * 4,
        shape(4, width, block // 4),
        *[shape(dp_n, seq_n, block)] * 2,
        *[shape(dp_n, 8, block // 4)] * 2,
        *[shape(seq_n, 8, block // 4)] * 2,
        shape(3 * width, block, dtype=BF16),
        *[shape(seq_n, chans, 2 * width)] * 4,
        *[shape(dp_n, 8, width // 2)] * 2,
        shape(8, width // 2),
        shape(seq_n, 8, width // 2),
        pltpu.SemaphoreType.DMA((12,)),
        pltpu.SemaphoreType.DMA((12,)),
    ]
    vmem = pl.BlockSpec(memory_space=pltpu.VMEM)
    out, dinp, gin, gout, gfil, gskip = pl.pallas_call(
        functools.partial(body, seq_n, dp_n, scale),
        out_shape=(
            jax.ShapeDtypeStruct((block, width), BF16),
            jax.ShapeDtypeStruct((block, width), BF16),
            jax.ShapeDtypeStruct((own, 3 * width), F32),
            jax.ShapeDtypeStruct((own, width), F32),
            jax.ShapeDtypeStruct((block, own), F32),
            jax.ShapeDtypeStruct((1, own), F32),
        ),
        in_specs=[vmem] * 7,
        out_specs=(vmem,) * 6,
        scratch_shapes=scratch,
        compiler_params=pltpu.CompilerParams(
            collective_id=0, has_side_effects=True, vmem_limit_bytes=56 * 1024 * 1024
        ),
        name="operator",
    )(tokens[0], cotangent[0], w_in, w_out, filter_taps, skip[None], jnp.asarray(tables(block)))
    return out[None], dinp[None], gin, gout, gfil, gskip[0]


def solution(mesh):
    return jax.shard_map(
        shards,
        mesh=mesh,
        in_specs=(P("dp", "seq", None), P("dp", "seq", None), P(), P(), P("seq", None), P()),
        out_specs=(
            P("dp", "seq", None),
            P("dp", "seq", None),
            P("dp", None),
            P("dp", None),
            P("seq", "dp"),
            P("dp"),
        ),
        check_vma=False,
    )
```

time: 746 us -> 88.4 us (0.12); the launches traced: 732 us -> 88.2 us
  waiting for transfers between devices: 273 us -> 0 us
  blocking collectives: 161 us -> 0 us
  matrix products: 119 us -> 0 us
  Pallas kernels: 0 us -> 81.9 us
  starting transfers between devices: 74.8 us -> 0 us
  local copies, waits for them, and re-layouts: 69.3 us -> 5.63 us
  other arithmetic: 18.7 us -> 0 us
  between operations: 15.4 us -> 0.66 us
    all_to_all x11 -> x0, waiting for transfers between devices: 194 us -> none  [the longest x4 91.7 us: regroup_spectral(): lax.all_to_all(signal, 'seq', split_axis=1, concat_axis=0, tiled=True)]
    psum x1 -> x0, blocking collectives: 124 us -> none  [shards(): in_sum, out_sum, skip_sum = lax.psum((in_term, out_term, skip_term), 'seq')]
    dot_general x22 -> x0, matrix products: 119 us -> none  [the longest x2 30.2 us: forward_spectrum(): jnp.einsum('kc,cjf->kjf', jnp.cos(inner_angle), spread, precision=HIGHEST)]
    pallas_call x0 -> x1, Pallas kernels: none -> 81.9 us  [shards(): pl.pallas_call(functools.partial(body, seq_n, dp_n, scale), out_shape=(ja...]
    all_to_all x11 -> x0, starting transfers between devices: 74.7 us -> none  [the longest x4 29.8 us: regroup_spectral(): lax.all_to_all(signal, 'seq', split_axis=1, concat_axis=0, tiled=True)]
    unnamed x6 -> x0, waiting for transfers between devices: 60.4 us -> none
    concatenate x6 -> x0, local copies, waits for them, and re-layouts: 28.4 us -> none  [the longest x2 11.5 us: inverse_field(): jnp.concatenate([cos_part[..., :chan_count] - sin_part[..., chan_count:],...]
    all_to_all x1 -> x0, blocking collectives: 24.4 us -> none  [regroup_real(): lax.all_to_all(signal, 'seq', split_axis=1, concat_axis=0, tiled=True)]
  transfers between devices with their start and end apart: 15 -> 0, of which waited for: 10 -> 0; matrix products, arithmetic and copies ran while one was open for 26% -> 0% of each run, Pallas kernels for 0% -> 0%
where the time goes in v1:
time: 88.4 us; the launch traced here: 88.2 us
  Pallas kernels  81.9 us (93%)
  local copies, waits for them, and re-layouts  5.63 us (6%)
    pallas_call x1, Pallas kernels, shards(): pl.pallas_call(functools.partial(body, seq_n, dp_n, scale), out_shape=(ja...  81.9 us
    unnamed x16, local copies, waits for them, and re-layouts  5.63 us

profile of v1, /device:TPU:1, one launch (start us, length us, event | category | flops | bytes accessed | tf_op | source)
XLA Modules:
  0.0 88.2 jit_solution(13560583657329253018)
XLA Ops:
  0.6 81.9 %operator.1 = (bf16[512,256]{1,0:T(8,128)(2,1)}, bf16[512,256]{1,0:T(8,128)(2,1)}, f32[32,768]{1,0:T(8,128)}, f32[32,256]{1,0:T(8,128)}, f32[512,32]{1,0:T(8,128)}, /*index=5*/f32[1,32]{1,0:T(1,128)}) custom-call(bf16[512,256]{1,0:T(8,128)(2,1)} %bitcast.6, bf16[512,256]{1,0:T(8,128)(2,1)} %bitcast.7, bf16[256,768]{1,0:T(8,128)(2,1)} %w_in.1, ...), custom_call_target="tpu_custom_call" | custom-call | tf_op jit(solution)/shard_map/operator/pallas_call | solution.py:412
  82.5 0.0 copy-start.1
  82.5 1.7 %copy.13 = f32[512,32]{0,1:T(8,128)} copy(f32[512,32]{1,0:T(8,128)} %get-tuple-element.22) | data formatting | bytes 131072
  84.3 0.0 copy-done.1
  84.3 0.0 copy-start
  84.3 0.7 copy.19
  85.0 0.3 copy-done
  85.3 0.0 copy-start.2
  85.3 0.7 copy.20
  86.0 0.3 copy-done.2
  86.3 0.0 copy-start.3
  86.3 0.6 copy.21
  86.9 0.1 copy-done.3
  87.0 0.0 copy-start.4
  87.0 0.6 copy.22
  87.7 0.0 copy-done.4
  87.7 0.5 copy.23
Async XLA Ops:
  82.5 1.7 %copy-start.1 = (bf16[512,256]{1,0:T(8,128)(2,1)S(1)}, bf16[512,256]{1,0:T(8,128)(2,1)}, u32[]{:S(2)}) copy-start(bf16[512,256]{1,0:T(8,128)(2,1)} %get-tuple-element.12) | copy-start | bytes 786436
  84.3 1.0 %copy-start = (bf16[512,256]{1,0:T(8,128)(2,1)S(1)}, bf16[512,256]{1,0:T(8,128)(2,1)}, u32[]{:S(2)}) copy-start(bf16[512,256]{1,0:T(8,128)(2,1)} %get-tuple-element.13) | copy-start | bytes 786436
  85.3 1.0 %copy-start.2 = (f32[32,768]{1,0:T(8,128)S(1)}, f32[32,768]{1,0:T(8,128)}, u32[]{:S(2)}) copy-start(f32[32,768]{1,0:T(8,128)} %get-tuple-element.32) | copy-start | bytes 294916
  86.3 0.8 copy-start.3
  87.0 0.6 copy-start.4

commit v2 on v1

--- a/solution.py
+++ b/solution.py
@@ -149,8 +149,12 @@
     dproj,
     g1_s,
     g2_s,
-    g1_r,
-    g2_r,
+    p1_r,
+    p2_r,
+    r1_s,
+    r2_s,
+    r1_r,
+    r2_r,
     z_s,
     z_r,
     a_s,
@@ -162,6 +166,7 @@
     chans = width // seq_n
     me = lax.axis_index("seq")
     my_dp = lax.axis_index("dp")
+    core = lax.rem(me, 2)
     group = 8 if seq_n >= 32 else 4
 
     barrier = pltpu.get_barrier_semaphore()
@@ -177,8 +182,8 @@
     lax.fori_loop(1, seq_n, greet_seq, 0)
     lax.fori_loop(1, dp_n, greet_dp, 0)
 
-    def exchange(src, dst, slot, axis="seq", gather=False):
-        mine, parts = (me, seq_n) if axis == "seq" else (my_dp, dp_n)
+    def exchange(src, dst, slot, axis="seq", gather=False, cores=1):
+        mine, parts = (me // cores, seq_n // cores) if axis == "seq" else (my_dp, dp_n)
         own = src if gather else src.at[mine]
         pltpu.make_async_copy(own, dst.at[mine], recv.at[slot]).start()
 
@@ -189,11 +194,20 @@
                 dst.at[mine],
                 send.at[slot],
                 recv.at[slot],
-                device_id={axis: peer},
+                device_id={axis: peer if cores == 1 else peer * cores + core},
             ).start()
             return 0
 
         lax.fori_loop(1, parts, go, 0)
+
+    def swap(src, dst, slot):
+        pltpu.make_async_remote_copy(
+            src.at[1 - core],
+            dst,
+            send.at[slot],
+            recv.at[slot],
+            device_id={"seq": me + 1 - 2 * core},
+        ).start()
 
     def arrived(dst, slot):
         pltpu.make_async_copy(dst, dst, recv.at[slot]).wait()
@@ -211,8 +225,6 @@
     high, low = split2(taps[...])
     taps_t = dot(perm, high, NT) + dot(perm, low, NT)
     tap_s[...] = taps_t.reshape(seq_n, chans, block)
-    pl.semaphore_wait(barrier, seq_n + dp_n - 2)
-    exchange(tap_s, tap_r, 0)
 
     for part in range(3):
         rows = pl.ds(part * width, width)
@@ -222,11 +234,13 @@
     gate_in = proj.at[pl.ds(width, width)]
     values = proj.at[pl.ds(2 * width, width)]
     gat_s[...] = (values[...] * gate_in[...]).reshape(seq_n, chans, block)
-    exchange(gat_s, gat_r, 1)
 
     w_o[...] = dot(perm, w_out[...]).astype(BF16)
     dmx[...] = dot(w_o[...], cot[...], NT)
     dcn_s[...] = (dmx[...] * gate_out[...]).reshape(seq_n, chans, block)
+    pl.semaphore_wait(barrier, seq_n + dp_n - 2)
+    exchange(tap_s, tap_r, 0)
+    exchange(gat_s, gat_r, 1)
     exchange(dcn_s, dcn_r, 2)
     tok_t[...] = dot(perm, tok[...], NT).astype(BF16)
 
@@ -316,10 +330,31 @@
     conv = con_r[...].reshape(width, block) + skip_col * gated
     mixed = (conv * gate_out[...]).astype(BF16)
     dproj[pl.ds(0, width), :] = (dmx[...] * conv).astype(BF16)
-    g1_s[:, :, :width] = dot(tok_t[...], dproj[pl.ds(0, width), :], NT).reshape(seq_n, chans, width)
-    g1_s[:, :, width:] = dot(mixed, cot[...]).reshape(seq_n, chans, width)
-    exchange(g1_s, g1_r, 7)
+
+    def fill(dst, first, term):
+        term = term.reshape(seq_n // 2, 2, chans, width)
+        for c in (0, 1):
+            dst[c, :, :, first : first + width] = term[:, c]
+
+    fill(g1_s, 0, dot(tok_t[...], dproj[pl.ds(0, width), :], NT))
+    fill(g1_s, width, dot(mixed, cot[...]))
+    swap(g1_s, p1_r, 7)
     out[...] = dot(mixed, w_o[...], TN).astype(BF16)
+    arrived(p1_r, 7)
+    r1_s[...] = g1_s[core] + p1_r[...]
+    exchange(r1_s, r1_r, 12, cores=2)
+
+    arrived(dga_r, 4)
+    dgated = dga_r[...].reshape(width, block) + skip_col * dcn_s[...].reshape(width, block)
+    dproj[pl.ds(width, width), :] = (dgated * values[...]).astype(BF16)
+    dproj[pl.ds(2 * width, width), :] = (dgated * gate_in[...]).astype(BF16)
+    for k in (0, 1):
+        fill(g2_s, k * width, dot(tok_t[...], dproj[pl.ds((k + 1) * width, width), :], NT))
+    swap(g2_s, p2_r, 9)
+    arrived(p2_r, 9)
+    r2_s[...] = g2_s[core] + p2_r[...]
+    exchange(r2_s, r2_r, 13, cores=2)
+    dinp[...] = dot(dproj[...], w_t[...], TN).astype(BF16)
 
     arrived(gf_r, 5)
     arrived(sk_r, 6)
@@ -330,30 +365,20 @@
     q_s[:, 4, :] = jnp.broadcast_to(sk_sum[0:1, :], (seq_n, lanes))
     exchange(q_s, q_r, 8)
 
-    arrived(dga_r, 4)
-    dgated = dga_r[...].reshape(width, block) + skip_col * dcn_s[...].reshape(width, block)
-    dproj[pl.ds(width, width), :] = (dgated * values[...]).astype(BF16)
-    dproj[pl.ds(2 * width, width), :] = (dgated * gate_in[...]).astype(BF16)
-    for k in (0, 1):
-        term = dot(tok_t[...], dproj[pl.ds((k + 1) * width, width), :], NT)
-        g2_s[:, :, k * width : (k + 1) * width] = term.reshape(seq_n, chans, width)
-    exchange(g2_s, g2_r, 9)
-    dinp[...] = dot(dproj[...], w_t[...], TN).astype(BF16)
-
-    arrived(q_r, 8)
-    for r in range(4):
-        gfil[r * lanes : (r + 1) * lanes, :] = q_r[:, r, :].T
-    gskip[...] = jnp.sum(q_r[:, 4, :].T, axis=0, keepdims=True)
-
-    arrived(g1_r, 7)
-    sum1 = jnp.sum(g1_r[...], axis=0) * scale
-    arrived(g2_r, 9)
-    sum2 = jnp.sum(g2_r[...], axis=0) * scale
+    arrived(r1_r, 12)
+    sum1 = jnp.sum(r1_r[...], axis=0) * scale
     piece = 2 * width // 4
     for r in range(4):
         z_s[:, r, :] = sum1[:, r * piece : (r + 1) * piece]
+    arrived(r2_r, 13)
+    sum2 = jnp.sum(r2_r[...], axis=0) * scale
+    for r in range(4):
         z_s[:, 4 + r, :] = sum2[:, r * piece : (r + 1) * piece]
     exchange(z_s, z_r, 10, "dp")
+    arrived(q_r, 8)
+    for r in range(4):
+        gfil[:, r * lanes : (r + 1) * lanes] = q_r[:, r, :]
+    gskip[...] = jnp.sum(q_r[:, 4, :].T, axis=0, keepdims=True)
     arrived(z_r, 10)
     a_s[...] = jnp.sum(z_r[...], axis=0)
     exchange(a_s, a_r, 11, gather=True)
@@ -367,10 +392,29 @@
         h, m, t = split3(line(r))
         gin[:, k * width : (k + 1) * width] = dot(h, perm) + (dot(m, perm) + dot(t, perm))
 
-    for slot, ref in enumerate(
-        (tap_r, gat_r, dcn_r, con_r, dga_r, gf_r, sk_r, g1_r, q_r, g2_r, z_r, a_r)
+    for slot, ref in (
+        (0, tap_r),
+        (1, gat_r),
+        (2, dcn_r),
+        (3, con_r),
+        (4, dga_r),
+        (5, gf_r),
+        (6, sk_r),
+        (8, q_r),
+        (10, z_r),
+        (11, a_r),
+        (12, r1_r),
+        (13, r2_r),
     ):
         sent(ref, slot)
+    for slot, ref in ((7, p1_r), (9, p2_r)):
+        pltpu.make_async_copy(ref, ref, send.at[slot]).wait()
+
+
+def deliver(*refs):
+    half = len(refs) // 2
+    for src, dst in zip(refs[:half], refs[half:]):
+        dst[...] = src[...]
 
 
 def shards(tokens, cotangent, w_in, w_out, filter_taps, skip):
@@ -401,22 +445,23 @@
         *[shape(dp_n, 8, block // 4)] * 2,
         *[shape(seq_n, 8, block // 4)] * 2,
         shape(3 * width, block, dtype=BF16),
-        *[shape(seq_n, chans, 2 * width)] * 4,
+        *[shape(2, seq_n // 2, chans, 2 * width)] * 2,
+        *[shape(seq_n // 2, chans, 2 * width)] * 6,
         *[shape(dp_n, 8, width // 2)] * 2,
         shape(8, width // 2),
         shape(seq_n, 8, width // 2),
-        pltpu.SemaphoreType.DMA((12,)),
-        pltpu.SemaphoreType.DMA((12,)),
+        pltpu.SemaphoreType.DMA((14,)),
+        pltpu.SemaphoreType.DMA((14,)),
     ]
     vmem = pl.BlockSpec(memory_space=pltpu.VMEM)
-    out, dinp, gin, gout, gfil, gskip = pl.pallas_call(
+    results = pl.pallas_call(
         functools.partial(body, seq_n, dp_n, scale),
         out_shape=(
             jax.ShapeDtypeStruct((block, width), BF16),
             jax.ShapeDtypeStruct((block, width), BF16),
             jax.ShapeDtypeStruct((own, 3 * width), F32),
             jax.ShapeDtypeStruct((own, width), F32),
-            jax.ShapeDtypeStruct((block, own), F32),
+            jax.ShapeDtypeStruct((own, block), F32),
             jax.ShapeDtypeStruct((1, own), F32),
         ),
         in_specs=[vmem] * 7,
@@ -427,7 +472,14 @@
         ),
         name="operator",
     )(tokens[0], cotangent[0], w_in, w_out, filter_taps, skip[None], jnp.asarray(tables(block)))
-    return out[None], dinp[None], gin, gout, gfil, gskip[0]
+    out, dinp, gin, gout, gfil, gskip = pl.pallas_call(
+        deliver,
+        out_shape=tuple(jax.ShapeDtypeStruct(r.shape, r.dtype) for r in results),
+        in_specs=[vmem] * 6,
+        out_specs=(vmem,) * 6,
+        name="deliver",
+    )(*results)
+    return out[None], dinp[None], gin, gout, gfil.T, gskip[0]
 
 
 def solution(mesh):

time: 88.4 us -> 75.5 us (0.85)
  Pallas kernels: 81.9 us -> 74.7 us
  local copies, waits for them, and re-layouts: 5.63 us -> 0 us
    pallas_call x1, Pallas kernels: 81.9 us -> 72.8 us  [shards(): pl.pallas_call(functools.partial(body, seq_n, dp_n, scale), out_shape=(ja...]
    unnamed x16 -> x0, local copies, waits for them, and re-layouts: 5.63 us -> none
    pallas_call x0 -> x1, Pallas kernels: none -> 1.94 us  [shards(): pl.pallas_call(deliver, out_shape=tuple((jax.ShapeDtypeStruct(r.shape, r....]
where the time goes in v2:
time: 75.5 us; the launch traced here: 75.4 us
  Pallas kernels  74.7 us (99%)
    pallas_call x1, Pallas kernels, shards(): pl.pallas_call(functools.partial(body, seq_n, dp_n, scale), out_shape=(ja...  72.8 us
    pallas_call x1, Pallas kernels, shards(): pl.pallas_call(deliver, out_shape=tuple((jax.ShapeDtypeStruct(r.shape, r....  1.94 us

profile of v2, /device:TPU:1, one launch (start us, length us, event | category | flops | bytes accessed | tf_op | source)
XLA Modules:
  0.0 75.4 jit_solution(2993309532244448633)
XLA Ops:
  0.6 72.8 %operator.1 = (bf16[512,256]{1,0:T(8,128)(2,1)}, bf16[512,256]{1,0:T(8,128)(2,1)}, f32[32,768]{1,0:T(8,128)}, f32[32,256]{1,0:T(8,128)}, f32[32,512]{1,0:T(8,128)}, /*index=5*/f32[1,32]{1,0:T(1,128)}) custom-call(bf16[512,256]{1,0:T(8,128)(2,1)} %bitcast.7, bf16[512,256]{1,0:T(8,128)(2,1)} %bitcast.8, bf16[256,768]{1,0:T(8,128)(2,1)} %w_in.1, ...), custom_call_target="tpu_custom_call" | custom-call | tf_op jit(solution)/shard_map/operator/pallas_call | solution.py:457
  73.4 1.9 %deliver.1 = (bf16[512,256]{1,0:T(8,128)(2,1)}, bf16[512,256]{1,0:T(8,128)(2,1)}, f32[32,768]{1,0:T(8,128)}, f32[32,256]{1,0:T(8,128)}, f32[32,512]{1,0:T(8,128)}, /*index=5*/f32[1,32]{1,0:T(1,128)}) custom-call(bf16[512,256]{1,0:T(8,128)(2,1)} %get-tuple-element.18.refs_0_, bf16[512,256]{1,0:T(8,128)(2,1)} %get-tuple-element.19.refs_1_, ...), custom_call_target="tpu_custom_call" | custom-call | tf_op jit(solution)/shard_map/deliver/pallas_call | solution.py:475

commit v3 on v2

--- a/solution.py
+++ b/solution.py
@@ -50,9 +50,8 @@
     return lax.dot_general(a, b, dims, preferred_element_type=F32)
 
 
-def block_conv(p_ref, q_ref, o_ref, block, size, corr):
-    count = q_ref.shape[0]
-    groups = count // size
+def block_conv(p_ref, q_ref, o_ref, block, size, corr, first, groups):
+    total = q_ref.shape[0] // size
     lanes = min(128, block)
 
     def tile(t, _):
@@ -65,40 +64,56 @@
             base = in0 - out0 if corr else out0 - in0
             for u in range(size):
                 qr, qi = q_ref[in0 + u, :, re], q_ref[in0 + u, :, im]
+                qs = qr + qi
                 for r in range(size):
                     lag = u - r if corr else r - u
                     if diag and lag < 0:
                         continue
                     if lag not in cache:
-                        cache[lag] = p_ref[base + lag, :, re], p_ref[base + lag, :, im]
-                    pr, pi = cache[lag]
-                    if corr:
-                        new_re, new_im = pr * qr + pi * qi, pr * qi - pi * qr
-                    else:
-                        new_re, new_im = pr * qr - pi * qi, pr * qi + pi * qr
-                    acc[2 * r] = acc[2 * r] + new_re
-                    acc[2 * r + 1] = acc[2 * r + 1] + new_im
+                        pr, pi = p_ref[base + lag, :, re], p_ref[base + lag, :, im]
+                        both, diff = pr + pi, pi - pr
+                        cache[lag] = (pr, -both, -diff) if corr else (pr, diff, both)
+                    one, two, three = cache[lag]
+                    acc[3 * r] = acc[3 * r] + one * qs
+                    acc[3 * r + 1] = acc[3 * r + 1] + two * qr
+                    acc[3 * r + 2] = acc[3 * r + 2] + three * qi
             return tuple(acc)
 
         def group(g, _):
             out0 = g * size
             zero = jnp.zeros((q_ref.shape[1], lanes), F32)
-            acc = chunk((zero,) * (2 * size), out0, out0, True)
+            acc = chunk((zero,) * (3 * size), out0, out0, True)
 
             def step(h, acc):
                 return chunk(acc, out0, h * size, False)
 
-            low, top = (g + 1, groups) if corr else (0, g)
+            low, top = (g + 1, total) if corr else (0, g)
             acc = lax.fori_loop(low, top, step, acc)
             for r in range(size):
-                o_ref[out0 + r, :, re] = acc[2 * r]
-                o_ref[out0 + r, :, im] = acc[2 * r + 1]
+                o_ref[out0 + r, :, re] = acc[3 * r] - acc[3 * r + 2]
+                o_ref[out0 + r, :, im] = acc[3 * r] + acc[3 * r + 1]
             return 0
 
-        lax.fori_loop(0, groups, group, 0)
+        lax.fori_loop(first, first + groups, group, 0)
         return 0
 
     lax.fori_loop(0, block // lanes, tile, 0)
+
+
+def farthest_first(step, mine, parts, ring):
+    if ring:
+        back = step % 2
+        return (mine + back * (parts - (step + 1) // 2) + (1 - back) * (step // 2)) % parts
+
+    def offset(i):
+        return (i * (i + 1) // 2) % 4
+
+    cores = parts // 16
+    if cores == 0:
+        return (mine + step) % parts
+    chip = mine // cores
+    x, y = chip // 4 + offset(step // (4 * cores)), chip % 4 + offset((step // cores) % 4)
+    return ((x % 4) * 4 + y % 4) * cores + (mine + step) % cores
 
 
 def body(
@@ -167,16 +182,18 @@
     me = lax.axis_index("seq")
     my_dp = lax.axis_index("dp")
     core = lax.rem(me, 2)
-    group = 8 if seq_n >= 32 else 4
+    group = 8 if seq_n >= 32 else 2
 
     barrier = pltpu.get_barrier_semaphore()
 
     def greet_seq(k, _):
-        pl.semaphore_signal(barrier, 1, device_id={"seq": lax.rem(me + k, seq_n)})
+        peer = farthest_first(seq_n - k, me, seq_n, False)
+        pl.semaphore_signal(barrier, 1, device_id={"seq": peer})
         return 0
 
     def greet_dp(k, _):
-        pl.semaphore_signal(barrier, 1, device_id={"dp": lax.rem(my_dp + k, dp_n)})
+        peer = farthest_first(dp_n - k, my_dp, dp_n, True)
+        pl.semaphore_signal(barrier, 1, device_id={"dp": peer})
         return 0
 
     lax.fori_loop(1, seq_n, greet_seq, 0)
@@ -188,7 +205,7 @@
         pltpu.make_async_copy(own, dst.at[mine], recv.at[slot]).start()
 
         def go(k, _):
-            peer = lax.rem(mine + k, parts)
+            peer = farthest_first(parts - k, mine, parts, axis == "dp")
             pltpu.make_async_remote_copy(
                 src if gather else src.at[peer],
                 dst.at[mine],
@@ -200,6 +217,30 @@
 
         lax.fori_loop(1, parts, go, 0)
 
+    half_n = seq_n // 2
+
+    def half_exchange(src, dst, slot, half, own):
+        if own:
+            pltpu.make_async_copy(src.at[me], dst.at[me], recv.at[slot]).start()
+
+        def go(k, _):
+            step = half_n - 1 - k
+            if half_n == 16:
+                x, y = (me // 8 + step // 8) % 2, (me // 2 + (step // 2) * (step // 2 + 1) // 2) % 4
+                peer = half * half_n + x * 8 + y * 2 + (me + step) % 2
+            else:
+                peer = half * half_n + (me + step) % half_n
+            pltpu.make_async_remote_copy(
+                src.at[peer],
+                dst.at[me],
+                send.at[slot],
+                recv.at[slot],
+                device_id={"seq": peer},
+            ).start()
+            return 0
+
+        lax.fori_loop(0, half_n - 1 if own else half_n, go, 0)
+
     def swap(src, dst, slot):
         pltpu.make_async_remote_copy(
             src.at[1 - core],
@@ -258,7 +299,7 @@
             at = pl.multiple_of(a * ROWS, ROWS)
             for k, value in enumerate((cos, sin)):
                 high, low = split2(value)
-                for copy, piece in enumerate((high, high, low)):
+                for copy, piece in enumerate((high, low) if vertical else (high, high, low)):
                     if vertical:
                         dst[pl.ds((2 * copy + k) * block + at, ROWS), :] = piece
                     else:
@@ -279,10 +320,11 @@
         for n in range(0, 2 * block, step):
             dst[:, :, n : n + step] = dot(wide, f_mat[:, n : n + step]).reshape(seq_n, chans, step)
 
-    def field(factor):
-        high, low = split2(o_sp[...].reshape(rows_n, 2 * block))
-        wide = jnp.concatenate([high, low, high], axis=1)
-        return dot(wide, b_mat[...]) * factor
+    def field(first, factor):
+        rows = half_n * chans
+        high, low = split2(o_sp[pl.ds(first, half_n)].reshape(rows, 2 * block))
+        wide = dot(jnp.concatenate([high, low], axis=0), b_mat[: 2 * block, :])
+        return (wide[:rows] + wide[rows:] + dot(high, b_mat[2 * block :, :])) * factor
 
     odd = lax.broadcasted_iota(jnp.int32, (1, 1, block), 2) % 2
     sign = (1 - 2 * odd).astype(F32)
@@ -295,34 +337,43 @@
 
     arrived(gat_r, 1)
     spectrum(gat_r, x_sp)
-    block_conv(h_sp, x_sp, o_sp, block, group, False)
-    con_s[...] = field(1.0 / block).reshape(seq_n, chans, block)
-    exchange(con_s, con_r, 3)
-
+    groups = half_n // group
+    mine = me // half_n
+
+    def send_back(q_sp, src, dst, slot, corr):
+        for own in (False, True):
+            half = mine if own else 1 - mine
+            first = half * half_n
+            block_conv(h_sp, q_sp, o_sp, block, group, corr, half * groups, groups)
+            src[pl.ds(first, half_n)] = field(first, 1.0 / block).reshape(half_n, chans, block)
+            half_exchange(src, dst, slot, half, own)
+
+    send_back(x_sp, con_s, con_r, 3, False)
     arrived(dcn_r, 2)
     spectrum(dcn_r, d_sp)
-    block_conv(h_sp, d_sp, o_sp, block, group, True)
-    dga_s[...] = field(1.0 / block).reshape(seq_n, chans, block)
-    exchange(dga_s, dga_r, 4)
-
-    block_conv(x_sp, d_sp, h_sp, block, group, True)
-    last = seq_n - 1
-    o_sp[last] = h_sp[last]
-    o_sp[:last, :, :block] = h_sp[:last, :, :block] + sign * h_sp[1:, :, block:]
-    o_sp[:last, :, block:] = h_sp[:last, :, block:] - sign * h_sp[1:, :, :block]
+    send_back(d_sp, dga_s, dga_r, 4, True)
+
     lanes = block // 4
-    term = field(scale / block)
-    for r in range(4):
-        gf_t[r] = term[:, r * lanes : (r + 1) * lanes]
-        for d in range(dp_n):
-            gf_s[d, :, r * lanes : (r + 1) * lanes] = gf_t[r, pl.ds(d, seq_n, stride=chans), :]
+    for half in (1, 0):
+        first, end = half * half_n, (half + 1) * half_n
+        block_conv(x_sp, d_sp, h_sp, block, group, True, half * groups, groups)
+        if half:
+            end = end - 1
+            o_sp[end] = h_sp[end]
+        o_sp[first:end, :, :block] = h_sp[first:end, :, :block] + sign * h_sp[first + 1 : end + 1, :, block:]
+        o_sp[first:end, :, block:] = h_sp[first:end, :, block:] - sign * h_sp[first + 1 : end + 1, :, :block]
+        term = field(first, scale / block)
+        for r in range(4):
+            gf_t[r] = term[:, r * lanes : (r + 1) * lanes]
+            for d in range(dp_n):
+                gf_s[half, d, :, r * lanes : (r + 1) * lanes] = gf_t[r, pl.ds(d, half_n, stride=chans), :]
+        exchange(gf_s.at[half], gf_r.at[half], 5 + 9 * half, "dp")
     both = jnp.sum(gat_r[...] * dcn_r[...], axis=0)
     narrow = both[:, :lanes]
     for r in range(1, 4):
         narrow = narrow + both[:, r * lanes : (r + 1) * lanes]
     for d in range(dp_n):
         sk_s[d] = jnp.broadcast_to(narrow[d : d + 1, :], (8, lanes))
-    exchange(gf_s, gf_r, 5, "dp")
     exchange(sk_s, sk_r, 6, "dp")
 
     arrived(con_r, 3)
@@ -356,12 +407,13 @@
     exchange(r2_s, r2_r, 13, cores=2)
     dinp[...] = dot(dproj[...], w_t[...], TN).astype(BF16)
 
-    arrived(gf_r, 5)
     arrived(sk_r, 6)
-    gf_sum = jnp.sum(gf_r[...], axis=0)
     sk_sum = jnp.sum(sk_r[...], axis=0) * scale
-    for r in range(4):
-        q_s[:, r, :] = gf_sum[:, r * lanes : (r + 1) * lanes]
+    for half in (1, 0):
+        arrived(gf_r.at[half], 5 + 9 * half)
+        gf_sum = jnp.sum(gf_r[half], axis=0)
+        for r in range(4):
+            q_s[half * half_n : (half + 1) * half_n, r, :] = gf_sum[:, r * lanes : (r + 1) * lanes]
     q_s[:, 4, :] = jnp.broadcast_to(sk_sum[0:1, :], (seq_n, lanes))
     exchange(q_s, q_r, 8)
 
@@ -398,7 +450,8 @@
         (2, dcn_r),
         (3, con_r),
         (4, dga_r),
-        (5, gf_r),
+        (5, gf_r.at[0]),
+        (14, gf_r.at[1]),
         (6, sk_r),
         (8, q_r),
         (10, z_r),
@@ -437,11 +490,11 @@
         shape(width, width, dtype=BF16),
         shape(width, block, dtype=BF16),
         shape(3 * block, 2 * block, dtype=BF16),
-        shape(6 * block, block, dtype=BF16),
+        shape(4 * block, block, dtype=BF16),
         *[shape(*sp)] * 4,
         *[shape(*ex)] * 4,
-        shape(4, width, block // 4),
-        *[shape(dp_n, seq_n, block)] * 2,
+        shape(4, width // 2, block // 4),
+        *[shape(2, dp_n, seq_n // 2, block)] * 2,
         *[shape(dp_n, 8, block // 4)] * 2,
         *[shape(seq_n, 8, block // 4)] * 2,
         shape(3 * width, block, dtype=BF16),
@@ -450,8 +503,8 @@
         *[shape(dp_n, 8, width // 2)] * 2,
         shape(8, width // 2),
         shape(seq_n, 8, width // 2),
-        pltpu.SemaphoreType.DMA((14,)),
-        pltpu.SemaphoreType.DMA((14,)),
+        pltpu.SemaphoreType.DMA((15,)),
+        pltpu.SemaphoreType.DMA((15,)),
     ]
     vmem = pl.BlockSpec(memory_space=pltpu.VMEM)
     results = pl.pallas_call(

time: 75.5 us -> 71.3 us (0.944)
  Pallas kernels: 74.7 us -> 70.6 us
    pallas_call x1, Pallas kernels: 72.8 us -> 68.6 us  [shards(): pl.pallas_call(functools.partial(body, seq_n, dp_n, scale), out_shape=(ja...]
where the time goes in v3:
time: 71.3 us; the launch traced here: 71.2 us
  Pallas kernels  70.6 us (99%)
    pallas_call x1, Pallas kernels, shards(): pl.pallas_call(functools.partial(body, seq_n, dp_n, scale), out_shape=(ja...  68.6 us
    pallas_call x1, Pallas kernels, shards(): pl.pallas_call(deliver, out_shape=tuple((jax.ShapeDtypeStruct(r.shape, r....  1.94 us

profile of v3, /device:TPU:1, one launch (start us, length us, event | category | flops | bytes accessed | tf_op | source)
XLA Modules:
  0.0 71.2 jit_solution(14414126534002857030)
XLA Ops:
  0.6 68.6 %operator.1 = (bf16[512,256]{1,0:T(8,128)(2,1)}, bf16[512,256]{1,0:T(8,128)(2,1)}, f32[32,768]{1,0:T(8,128)}, f32[32,256]{1,0:T(8,128)}, f32[32,512]{1,0:T(8,128)}, /*index=5*/f32[1,32]{1,0:T(1,128)}) custom-call(bf16[512,256]{1,0:T(8,128)(2,1)} %bitcast.7, bf16[512,256]{1,0:T(8,128)(2,1)} %bitcast.8, bf16[256,768]{1,0:T(8,128)(2,1)} %w_in.1, ...), custom_call_target="tpu_custom_call" | custom-call | tf_op jit(solution)/shard_map/operator/pallas_call | solution.py:510
  69.2 1.9 %deliver.1 = (bf16[512,256]{1,0:T(8,128)(2,1)}, bf16[512,256]{1,0:T(8,128)(2,1)}, f32[32,768]{1,0:T(8,128)}, f32[32,256]{1,0:T(8,128)}, f32[32,512]{1,0:T(8,128)}, /*index=5*/f32[1,32]{1,0:T(1,128)}) custom-call(bf16[512,256]{1,0:T(8,128)(2,1)} %get-tuple-element.18.refs_0_, bf16[512,256]{1,0:T(8,128)(2,1)} %get-tuple-element.19.refs_1_, ...), custom_call_target="tpu_custom_call" | custom-call | tf_op jit(solution)/shard_map/deliver/pallas_call | solution.py:528

commit v4 on v3

--- a/solution.py
+++ b/solution.py
@@ -261,29 +261,34 @@
     col = lax.broadcasted_iota(jnp.int32, (width, width), 1)
     hit = (col % seq_n) * chans + col // seq_n == row
     perm = jnp.where(hit, 1.0, 0.0).astype(BF16)
-    skip_col = jnp.sum(jnp.where(hit, skip[...], 0.0), axis=1, keepdims=True)
-
-    high, low = split2(taps[...])
-    taps_t = dot(perm, high, NT) + dot(perm, low, NT)
-    tap_s[...] = taps_t.reshape(seq_n, chans, block)
 
     for part in range(3):
         rows = pl.ds(part * width, width)
         w_t[rows, :] = dot(perm, w_in[:, part * width : (part + 1) * width], NT).astype(BF16)
-        proj[rows, :] = dot(w_t[rows, :], tok[...], NT)
+    high, low = split2(taps[...])
+    taps_t = dot(perm, high, NT) + dot(perm, low, NT)
+    for h in (0, 1):
+        piece = taps_t[:, h * (block // 2) : (h + 1) * (block // 2)]
+        tap_s[h] = piece.reshape(seq_n, chans, block // 2)
     gate_out = proj.at[pl.ds(0, width)]
     gate_in = proj.at[pl.ds(width, width)]
     values = proj.at[pl.ds(2 * width, width)]
+    gate_in[...] = dot(w_t[pl.ds(width, width), :], tok[...], NT)
+    values[...] = dot(w_t[pl.ds(2 * width, width), :], tok[...], NT)
     gat_s[...] = (values[...] * gate_in[...]).reshape(seq_n, chans, block)
-
+    pl.semaphore_wait(barrier, seq_n + dp_n - 2)
+
+    parity = my_dp % 2
+    near, far = tap_r.at[parity], tap_r.at[1 - parity]
+    exchange(tap_s.at[parity], near, 0)
+    exchange(gat_s, gat_r, 1)
+    gate_out[...] = dot(w_t[pl.ds(0, width), :], tok[...], NT)
     w_o[...] = dot(perm, w_out[...]).astype(BF16)
     dmx[...] = dot(w_o[...], cot[...], NT)
     dcn_s[...] = (dmx[...] * gate_out[...]).reshape(seq_n, chans, block)
-    pl.semaphore_wait(barrier, seq_n + dp_n - 2)
-    exchange(tap_s, tap_r, 0)
-    exchange(gat_s, gat_r, 1)
     exchange(dcn_s, dcn_r, 2)
     tok_t[...] = dot(perm, tok[...], NT).astype(BF16)
+    skip_col = jnp.sum(jnp.where(hit, skip[...], 0.0), axis=1, keepdims=True)
 
     big = block // ROWS
 
@@ -309,13 +314,19 @@
         lax.fori_loop(0, big, rows_of, 0)
 
     build(f_mat, 0, False)
+    arrived(near, 0)
+    for low, side in ((0, 1), (half_n, dp_n - 1)):
+        piece = near.at[pl.ds(low, half_n)]
+        pltpu.make_async_remote_copy(
+            piece, piece, send.at[15], recv.at[15], device_id={"dp": (my_dp + side) % dp_n}
+        ).start()
     build(b_mat, 2 * big + 2 * ROWS, True)
 
     rows_n = seq_n * chans
     step = min(256, block)
 
     def spectrum(src, dst):
-        high, low = split2(src[...].reshape(rows_n, block))
+        high, low = split2(src.reshape(rows_n, block))
         wide = jnp.concatenate([high, low, high], axis=1)
         for n in range(0, 2 * block, step):
             dst[:, :, n : n + step] = dot(wide, f_mat[:, n : n + step]).reshape(seq_n, chans, step)
@@ -329,14 +340,14 @@
     odd = lax.broadcasted_iota(jnp.int32, (1, 1, block), 2) % 2
     sign = (1 - 2 * odd).astype(F32)
 
-    arrived(tap_r, 0)
-    spectrum(tap_r, o_sp)
+    arrived(gat_r, 1)
+    spectrum(gat_r[...], x_sp)
+    arrived(far, 15)
+    spectrum(jnp.concatenate([tap_r[0], tap_r[1]], axis=2), o_sp)
     h_sp[0] = o_sp[0]
     h_sp[1:, :, :block] = o_sp[1:, :, :block] - sign * o_sp[: seq_n - 1, :, block:]
     h_sp[1:, :, block:] = o_sp[1:, :, block:] + sign * o_sp[: seq_n - 1, :, :block]
 
-    arrived(gat_r, 1)
-    spectrum(gat_r, x_sp)
     groups = half_n // group
     mine = me // half_n
 
@@ -350,7 +361,7 @@
 
     send_back(x_sp, con_s, con_r, 3, False)
     arrived(dcn_r, 2)
-    spectrum(dcn_r, d_sp)
+    spectrum(dcn_r[...], d_sp)
     send_back(d_sp, dga_s, dga_r, 4, True)
 
     lanes = block // 4
@@ -445,7 +456,7 @@
         gin[:, k * width : (k + 1) * width] = dot(h, perm) + (dot(m, perm) + dot(t, perm))
 
     for slot, ref in (
-        (0, tap_r),
+        (0, near),
         (1, gat_r),
         (2, dcn_r),
         (3, con_r),
@@ -460,7 +471,7 @@
         (13, r2_r),
     ):
         sent(ref, slot)
-    for slot, ref in ((7, p1_r), (9, p2_r)):
+    for slot, ref in ((7, p1_r), (9, p2_r), (15, near)):
         pltpu.make_async_copy(ref, ref, send.at[slot]).wait()
 
 
@@ -483,7 +494,10 @@
     ex = (seq_n, chans, block)
     sp = (seq_n, chans, 2 * block)
     scratch = [
-        *[shape(*ex)] * 6,
+        shape(2, seq_n, chans, block // 2),
+        *[shape(*ex)] * 2,
+        shape(2, seq_n, chans, block // 2),
+        *[shape(*ex)] * 2,
         shape(3 * width, block),
         shape(width, block),
         shape(3 * width, width, dtype=BF16),
@@ -503,10 +517,11 @@
         *[shape(dp_n, 8, width // 2)] * 2,
         shape(8, width // 2),
         shape(seq_n, 8, width // 2),
-        pltpu.SemaphoreType.DMA((15,)),
-        pltpu.SemaphoreType.DMA((15,)),
+        pltpu.SemaphoreType.DMA((16,)),
+        pltpu.SemaphoreType.DMA((16,)),
     ]
     vmem = pl.BlockSpec(memory_space=pltpu.VMEM)
+    anywhere = pl.BlockSpec(memory_space=pl.ANY)
     results = pl.pallas_call(
         functools.partial(body, seq_n, dp_n, scale),
         out_shape=(

time: 71.3 us -> 69.7 us (0.978)
  Pallas kernels: 70.6 us -> 68.9 us
    pallas_call x1, Pallas kernels: 68.6 us -> 67 us  [shards(): pl.pallas_call(functools.partial(body, seq_n, dp_n, scale), out_shape=(ja...]
where the time goes in v4:
time: 69.7 us; the launch traced here: 69.6 us
  Pallas kernels  68.9 us (99%)
    pallas_call x1, Pallas kernels, shards(): pl.pallas_call(functools.partial(body, seq_n, dp_n, scale), out_shape=(ja...  67 us
    pallas_call x1, Pallas kernels, shards(): pl.pallas_call(deliver, out_shape=tuple((jax.ShapeDtypeStruct(r.shape, r....  1.94 us

profile of v4, /device:TPU:1, one launch (start us, length us, event | category | flops | bytes accessed | tf_op | source)
XLA Modules:
  0.0 69.6 jit_solution(10307847140602537163)
XLA Ops:
  0.6 67.0 %operator.1 = (bf16[512,256]{1,0:T(8,128)(2,1)}, bf16[512,256]{1,0:T(8,128)(2,1)}, f32[32,768]{1,0:T(8,128)}, f32[32,256]{1,0:T(8,128)}, f32[32,512]{1,0:T(8,128)}, /*index=5*/f32[1,32]{1,0:T(1,128)}) custom-call(bf16[512,256]{1,0:T(8,128)(2,1)} %bitcast.7, bf16[512,256]{1,0:T(8,128)(2,1)} %bitcast.8, bf16[256,768]{1,0:T(8,128)(2,1)} %w_in.1, ...), custom_call_target="tpu_custom_call" | custom-call | tf_op jit(solution)/shard_map/operator/pallas_call | solution.py:525
  67.6 1.9 %deliver.1 = (bf16[512,256]{1,0:T(8,128)(2,1)}, bf16[512,256]{1,0:T(8,128)(2,1)}, f32[32,768]{1,0:T(8,128)}, f32[32,256]{1,0:T(8,128)}, f32[32,512]{1,0:T(8,128)}, /*index=5*/f32[1,32]{1,0:T(1,128)}) custom-call(bf16[512,256]{1,0:T(8,128)(2,1)} %get-tuple-element.18.refs_0_, bf16[512,256]{1,0:T(8,128)(2,1)} %get-tuple-element.19.refs_1_, ...), custom_call_target="tpu_custom_call" | custom-call | tf_op jit(solution)/shard_map/deliver/pallas_call | solution.py:543

commit v5 on v4

--- a/solution.py
+++ b/solution.py
@@ -262,25 +262,25 @@
     hit = (col % seq_n) * chans + col // seq_n == row
     perm = jnp.where(hit, 1.0, 0.0).astype(BF16)
 
-    for part in range(3):
-        rows = pl.ds(part * width, width)
-        w_t[rows, :] = dot(perm, w_in[:, part * width : (part + 1) * width], NT).astype(BF16)
     high, low = split2(taps[...])
     taps_t = dot(perm, high, NT) + dot(perm, low, NT)
     for h in (0, 1):
         piece = taps_t[:, h * (block // 2) : (h + 1) * (block // 2)]
         tap_s[h] = piece.reshape(seq_n, chans, block // 2)
+    pl.semaphore_wait(barrier, seq_n + dp_n - 2)
+
+    parity = my_dp % 2
+    near, far = tap_r.at[parity], tap_r.at[1 - parity]
+    exchange(tap_s.at[parity], near, 0)
+    for part in range(3):
+        rows = pl.ds(part * width, width)
+        w_t[rows, :] = dot(perm, w_in[:, part * width : (part + 1) * width], NT).astype(BF16)
     gate_out = proj.at[pl.ds(0, width)]
     gate_in = proj.at[pl.ds(width, width)]
     values = proj.at[pl.ds(2 * width, width)]
     gate_in[...] = dot(w_t[pl.ds(width, width), :], tok[...], NT)
     values[...] = dot(w_t[pl.ds(2 * width, width), :], tok[...], NT)
     gat_s[...] = (values[...] * gate_in[...]).reshape(seq_n, chans, block)
-    pl.semaphore_wait(barrier, seq_n + dp_n - 2)
-
-    parity = my_dp % 2
-    near, far = tap_r.at[parity], tap_r.at[1 - parity]
-    exchange(tap_s.at[parity], near, 0)
     exchange(gat_s, gat_r, 1)
     gate_out[...] = dot(w_t[pl.ds(0, width), :], tok[...], NT)
     w_o[...] = dot(perm, w_out[...]).astype(BF16)
@@ -418,16 +418,6 @@
     exchange(r2_s, r2_r, 13, cores=2)
     dinp[...] = dot(dproj[...], w_t[...], TN).astype(BF16)
 
-    arrived(sk_r, 6)
-    sk_sum = jnp.sum(sk_r[...], axis=0) * scale
-    for half in (1, 0):
-        arrived(gf_r.at[half], 5 + 9 * half)
-        gf_sum = jnp.sum(gf_r[half], axis=0)
-        for r in range(4):
-            q_s[half * half_n : (half + 1) * half_n, r, :] = gf_sum[:, r * lanes : (r + 1) * lanes]
-    q_s[:, 4, :] = jnp.broadcast_to(sk_sum[0:1, :], (seq_n, lanes))
-    exchange(q_s, q_r, 8)
-
     arrived(r1_r, 12)
     sum1 = jnp.sum(r1_r[...], axis=0) * scale
     piece = 2 * width // 4
@@ -438,13 +428,23 @@
     for r in range(4):
         z_s[:, 4 + r, :] = sum2[:, r * piece : (r + 1) * piece]
     exchange(z_s, z_r, 10, "dp")
+    arrived(sk_r, 6)
+    sk_sum = jnp.sum(sk_r[...], axis=0) * scale
+    for half in (1, 0):
+        arrived(gf_r.at[half], 5 + 9 * half)
+        gf_sum = jnp.sum(gf_r[half], axis=0)
+        for r in range(4):
+            q_s[half * half_n : (half + 1) * half_n, r, :] = gf_sum[:, r * lanes : (r + 1) * lanes]
+    q_s[:, 4, :] = jnp.broadcast_to(sk_sum[0:1, :], (seq_n, lanes))
+    exchange(q_s, q_r, 8)
+
+    arrived(z_r, 10)
+    a_s[...] = jnp.sum(z_r[...], axis=0)
+    exchange(a_s, a_r, 11, gather=True)
     arrived(q_r, 8)
     for r in range(4):
         gfil[:, r * lanes : (r + 1) * lanes] = q_r[:, r, :]
     gskip[...] = jnp.sum(q_r[:, 4, :].T, axis=0, keepdims=True)
-    arrived(z_r, 10)
-    a_s[...] = jnp.sum(z_r[...], axis=0)
-    exchange(a_s, a_r, 11, gather=True)
     arrived(a_r, 11)
 
     def line(r):

time: 69.7 us -> 67.5 us (0.968)
  Pallas kernels: 68.9 us -> 66.7 us
    pallas_call x1, Pallas kernels: 67 us -> 64.8 us  [shards(): pl.pallas_call(functools.partial(body, seq_n, dp_n, scale), out_shape=(ja...]
where the time goes in v5:
time: 67.5 us; the launch traced here: 67.4 us
  Pallas kernels  66.7 us (99%)
    pallas_call x1, Pallas kernels, shards(): pl.pallas_call(functools.partial(body, seq_n, dp_n, scale), out_shape=(ja...  64.8 us
    pallas_call x1, Pallas kernels, shards(): pl.pallas_call(deliver, out_shape=tuple((jax.ShapeDtypeStruct(r.shape, r....  1.94 us

profile of v5, /device:TPU:1, one launch (start us, length us, event | category | flops | bytes accessed | tf_op | source)
XLA Modules:
  0.0 67.4 jit_solution(17150537315934033801)
XLA Ops:
  0.6 64.8 %operator.1 = (bf16[512,256]{1,0:T(8,128)(2,1)}, bf16[512,256]{1,0:T(8,128)(2,1)}, f32[32,768]{1,0:T(8,128)}, f32[32,256]{1,0:T(8,128)}, f32[32,512]{1,0:T(8,128)}, /*index=5*/f32[1,32]{1,0:T(1,128)}) custom-call(bf16[512,256]{1,0:T(8,128)(2,1)} %bitcast.7, bf16[512,256]{1,0:T(8,128)(2,1)} %bitcast.8, bf16[256,768]{1,0:T(8,128)(2,1)} %w_in.1, ...), custom_call_target="tpu_custom_call" | custom-call | tf_op jit(solution)/shard_map/operator/pallas_call | solution.py:525
  65.4 1.9 %deliver.1 = (bf16[512,256]{1,0:T(8,128)(2,1)}, bf16[512,256]{1,0:T(8,128)(2,1)}, f32[32,768]{1,0:T(8,128)}, f32[32,256]{1,0:T(8,128)}, f32[32,512]{1,0:T(8,128)}, /*index=5*/f32[1,32]{1,0:T(1,128)}) custom-call(bf16[512,256]{1,0:T(8,128)(2,1)} %get-tuple-element.18.refs_0_, bf16[512,256]{1,0:T(8,128)(2,1)} %get-tuple-element.19.refs_1_, ...), custom_call_target="tpu_custom_call" | custom-call | tf_op jit(solution)/shard_map/deliver/pallas_call | solution.py:543

commit v6 on v5

--- a/solution.py
+++ b/solution.py
@@ -379,6 +379,20 @@
             for d in range(dp_n):
                 gf_s[half, d, :, r * lanes : (r + 1) * lanes] = gf_t[r, pl.ds(d, half_n, stride=chans), :]
         exchange(gf_s.at[half], gf_r.at[half], 5 + 9 * half, "dp")
+    arrived(con_r, 3)
+    gated = gat_s[...].reshape(width, block)
+    conv = con_r[...].reshape(width, block) + skip_col * gated
+    mixed = (conv * gate_out[...]).astype(BF16)
+    dproj[pl.ds(0, width), :] = (dmx[...] * conv).astype(BF16)
+
+    def fill(dst, first, term):
+        term = term.reshape(seq_n // 2, 2, chans, width)
+        for c in (0, 1):
+            dst[c, :, :, first : first + width] = term[:, c]
+
+    fill(g1_s, 0, dot(tok_t[...], dproj[pl.ds(0, width), :], NT))
+    fill(g1_s, width, dot(mixed, cot[...]))
+    swap(g1_s, p1_r, 7)
     both = jnp.sum(gat_r[...] * dcn_r[...], axis=0)
     narrow = both[:, :lanes]
     for r in range(1, 4):
@@ -386,22 +400,6 @@
     for d in range(dp_n):
         sk_s[d] = jnp.broadcast_to(narrow[d : d + 1, :], (8, lanes))
     exchange(sk_s, sk_r, 6, "dp")
-
-    arrived(con_r, 3)
-    gated = gat_s[...].reshape(width, block)
-    conv = con_r[...].reshape(width, block) + skip_col * gated
-    mixed = (conv * gate_out[...]).astype(BF16)
-    dproj[pl.ds(0, width), :] = (dmx[...] * conv).astype(BF16)
-
-    def fill(dst, first, term):
-        term = term.reshape(seq_n // 2, 2, chans, width)
-        for c in (0, 1):
-            dst[c, :, :, first : first + width] = term[:, c]
-
-    fill(g1_s, 0, dot(tok_t[...], dproj[pl.ds(0, width), :], NT))
-    fill(g1_s, width, dot(mixed, cot[...]))
-    swap(g1_s, p1_r, 7)
-    out[...] = dot(mixed, w_o[...], TN).astype(BF16)
     arrived(p1_r, 7)
     r1_s[...] = g1_s[core] + p1_r[...]
     exchange(r1_s, r1_r, 12, cores=2)
@@ -416,6 +414,7 @@
     arrived(p2_r, 9)
     r2_s[...] = g2_s[core] + p2_r[...]
     exchange(r2_s, r2_r, 13, cores=2)
+    out[...] = dot(mixed, w_o[...], TN).astype(BF16)
     dinp[...] = dot(dproj[...], w_t[...], TN).astype(BF16)
 
     arrived(r1_r, 12)

time: 67.5 us -> 67.2 us (level)
  no operation moved by 1% of the time
where the time goes in v6:
time: 67.2 us; the launch traced here: 67.1 us
  Pallas kernels  66.4 us (99%)
    pallas_call x1, Pallas kernels, shards(): pl.pallas_call(functools.partial(body, seq_n, dp_n, scale), out_shape=(ja...  64.5 us
    pallas_call x1, Pallas kernels, shards(): pl.pallas_call(deliver, out_shape=tuple((jax.ShapeDtypeStruct(r.shape, r....  1.94 us

profile of v6, /device:TPU:1, one launch (start us, length us, event | category | flops | bytes accessed | tf_op | source)
XLA Modules:
  0.0 67.1 jit_solution(1493040757802273642)
XLA Ops:
  0.6 64.5 %operator.1 = (bf16[512,256]{1,0:T(8,128)(2,1)}, bf16[512,256]{1,0:T(8,128)(2,1)}, f32[32,768]{1,0:T(8,128)}, f32[32,256]{1,0:T(8,128)}, f32[32,512]{1,0:T(8,128)}, /*index=5*/f32[1,32]{1,0:T(1,128)}) custom-call(bf16[512,256]{1,0:T(8,128)(2,1)} %bitcast.7, bf16[512,256]{1,0:T(8,128)(2,1)} %bitcast.8, bf16[256,768]{1,0:T(8,128)(2,1)} %w_in.1, ...), custom_call_target="tpu_custom_call" | custom-call | tf_op jit(solution)/shard_map/operator/pallas_call | solution.py:524
  65.1 1.9 %deliver.1 = (bf16[512,256]{1,0:T(8,128)(2,1)}, bf16[512,256]{1,0:T(8,128)(2,1)}, f32[32,768]{1,0:T(8,128)}, f32[32,256]{1,0:T(8,128)}, f32[32,512]{1,0:T(8,128)}, /*index=5*/f32[1,32]{1,0:T(1,128)}) custom-call(bf16[512,256]{1,0:T(8,128)(2,1)} %get-tuple-element.18.refs_0_, bf16[512,256]{1,0:T(8,128)(2,1)} %get-tuple-element.19.refs_1_, ...), custom_call_target="tpu_custom_call" | custom-call | tf_op jit(solution)/shard_map/deliver/pallas_call | solution.py:542
